TPU v7x, 32 devices: a whole 2x2x4 slice. The times are simulated.
32 devices in a mesh: dom: 8 (over z, y), rep: 4 (over x, core).
Axes of the slice: x: 2, y: 2, z: 4, core: 2. Of those that a mesh axis runs over, the one named last changes fastest.
Arguments:
- feats: bfloat16 [256, 32768], P('rep', 'dom'), may hold values from -6 to 6
- w_self: bfloat16 [256, 256], P(None, 'rep'), may hold values from -0.375 to 0.375
- w_neigh: bfloat16 [256, 256], P(None, 'rep'), may hold values from -3 to 3
- local_cols: int32 [256, 2], P('dom'), may hold values from 0 to 31
- local_tiles: bfloat16 [256, 2, 128, 128], P('dom'), may hold values from 0 to 3, as said below
- send_list: int32 [8, 8, 2], P('dom'), may hold values from 0 to 31
- remote_rows: int32 [8, 8, 2], P('dom'), may hold values from 0 to 31
- remote_tiles: bfloat16 [8, 8, 2, 128, 128], P('dom'), may hold values from 0 to 3, as said below
- cotangent: bfloat16 [256, 32768], P('rep', 'dom'), may hold values from -6 to 6
Outputs:
- output: bfloat16 [256, 32768], P('rep', 'dom')
- grad_feats: bfloat16 [256, 32768], P('rep', 'dom')
- grad_w_self: float32 [256, 256], P(None, 'rep')
- grad_w_neigh: float32 [256, 256], P(None, 'rep')
Inputs may be any that keep to these rules, and one draw needn't show every extreme that they name: `local_tiles`: edge weights: zero where a tile has no edge, positive otherwise. `remote_tiles`: edge weights: zero where a tile has no edge, positive otherwise.
All inputs are finite; a program needn't handle non-finite values.
Results may differ from a plain program's by a relative error of at most 0.0055.
Values may be sent and summed in bfloat16 or wider, within the bound.
A program may use at most 128 MiB of HBM per device.

v0:
```python
import functools

import jax
import jax.numpy as jnp
from jax import lax
from jax.experimental import pallas as pl
from jax.experimental.pallas import tpu as pltpu
from jax.sharding import PartitionSpec as P

MESH = pl.DeviceIdType.MESH
F32 = jnp.float32
BF16 = jnp.bfloat16
CHUNKS = 4
ONES = 16
KEEP = 8
NT = (((1,), (1,)), ((), ()))


def mm(a, b):
    return jnp.dot(a, b, preferred_element_type=F32)


def mm_nt(a, b):
    return lax.dot_general(a, b, NT, preferred_element_type=F32)


def equal_one(x, y):
    gap = x - y
    return (1 - jnp.minimum(gap * gap, 1)).astype(F32)


def rcopy(src, dst, send, recv, dom, rep):
    return pltpu.make_async_remote_copy(
        src_ref=src,
        dst_ref=dst,
        send_sem=send,
        recv_sem=recv,
        device_id={"dom": dom, "rep": rep},
        device_id_type=MESH,
    )


def greet(devices):
    barrier = pltpu.get_barrier_semaphore()
    for dom, rep in devices:
        pl.semaphore_signal(
            barrier, inc=1, device_id={"dom": dom, "rep": rep}, device_id_type=MESH
        )
    pl.semaphore_wait(barrier, len(devices))


def main_kernel(
    D,
    R,
    feats,
    wts_in,
    wtn_in,
    cols,
    slist,
    rrows,
    ltiles_h,
    rtiles_h,
    cot_h,
    out_o,
    acc_o,
    back_o,
    final_o,
    ltiles,
    rtiles,
    cot,
    blocks_of,
    hsend,
    hrecv,
    summed,
    far,
    inv,
    wts,
    wtn,
    wb,
    xf,
    xa,
    own,
    psend,
    precv,
    gp,
    gw,
    gpart,
    red,
    scaled,
    ret,
    nearb,
    loc_sem,
    h_s,
    h_r,
    ws_s,
    ws_r,
    wn_s,
    wn_r,
    xf_s,
    xf_r,
    xa_s,
    xa_r,
    pp_s,
    pp_r,
    gx_s,
    gx_r,
    gc_s,
    gc_r,
    b_s,
    b_r,
    p_s,
    p_r,
    f_s,
    f_r,
):
    d, r = lax.axis_index("dom"), lax.axis_index("rep")
    G = R // 2
    c, g = lax.rem(r, 2), lax.div(r, 2)
    mate = g * 2 + 1 - c
    F, N = feats.shape
    B, L, T, _ = ltiles.shape
    K = slist.shape[0]
    CH = N // CHUNKS
    CB = B // CHUNKS

    def cross(q):
        return lax.rem(g + q, G) * 2 + c

    loads = [
        pltpu.make_async_copy(ltiles_h, ltiles, loc_sem.at[0]),
        pltpu.make_async_copy(rtiles_h, rtiles, loc_sem.at[1]),
        pltpu.make_async_copy(cot_h, cot, loc_sem.at[2]),
    ]
    for load in loads:
        load.start()
    for b in range(B):
        blocks_of[b] = feats[:, b * T : (b + 1) * T]
    greet(
        [
            (lax.rem(d + p, D), cross(q))
            for q in range(G)
            for p in range(D)
            if p or q
        ]
        + [(d, lax.rem(g + q, G) * 2 + 1 - c) for q in range(G)]
    )

    def halo(p):
        return rcopy(
            hsend.at[p], hrecv.at[p], h_s.at[p], h_r.at[p], lax.rem(d + p, D), r
        )

    def pick(p, dst):
        for k in range(K):
            dst[p, k] = blocks_of[slist[k, lax.rem(d + p, D)]]

    def send_halo(p, carry):
        pick(p, hsend)
        halo(p).start()
        return carry

    lax.fori_loop(1, D, send_halo, 0)
    pick(0, hrecv)
    weight_copies, cross_weights = [], []
    sets = ((wts_in, wts, ws_s, ws_r), (wtn_in, wtn, wn_s, wn_r))
    chip = pl.ds(pl.multiple_of(g * 2 * F, 2 * F), 2 * F)
    for q in range(1, G):
        there = lax.rem(g + q, G)
        cut = pl.ds(pl.multiple_of(there * 2 * F, 2 * F), 2 * F)
        for src, dst, ss, rs in sets:
            cross_weights.append(
                rcopy(src.at[:, cut], dst.at[r], ss.at[q], rs.at[q], d, cross(q))
            )
    for src, dst, ss, rs in sets:
        weight_copies.append(
            rcopy(src.at[:, chip], dst.at[r], ss.at[0], rs.at[0], d, mate)
        )
    for copy in cross_weights + weight_copies:
        copy.start()
    feat_copy = rcopy(feats, xf.at[c], xf_s, xf_r, d, mate)
    feat_copy.start()
    wts[r] = wts_in[:, chip]
    wtn[r] = wtn_in[:, chip]
    xf[c] = feats[...]

    ones = jnp.ones((ONES, T), BF16)
    ones_wide = jnp.ones((ONES, L * T), BF16)
    loads[0].wait()

    def near(b, carry):
        left = jnp.concatenate(
            [
                blocks_of[cols[l, b]]
                for l in range(L)
            ],
            axis=1,
        )
        left = jnp.concatenate([left, ones_wide], axis=0)
        right = jnp.concatenate([ltiles[b, l] for l in range(L)], axis=1)
        summed[b] = mm_nt(left, right)[: F + KEEP]
        return carry

    lax.fori_loop(0, B, near, 0, unroll=4)
    for copy in cross_weights:
        copy.wait_recv()
    for q in range(1, G):
        t = lax.rem(g - q + G, G) * 2 + c
        for _, dst, ss, rs in sets:
            slot = G + q - 1
            copy = rcopy(dst.at[t], dst.at[t], ss.at[slot], rs.at[slot], d, mate)
            copy.start()
            weight_copies.append(copy)
    loads[1].wait()

    def far_step(p, carry):
        source = lax.rem(d - p + D, D)
        for k in range(K):
            left = jnp.concatenate([hrecv[p, k], ones], axis=0)
            far[p * K + k] = mm_nt(left, rtiles[source, k])[: F + KEEP]
        return carry

    def far_wait(p, carry):
        halo(p).wait_recv()
        return carry

    far_step(0, 0)
    lax.fori_loop(1, D, far_wait, 0)
    lax.fori_loop(1, D, far_step, 0, unroll=7)

    agg_copies = []
    for ch in range(CHUNKS):

        def place(i, carry):
            b = ch * CB + i
            total = summed[b]

            def add(p, total):
                source = lax.rem(d - p + D, D)
                for k in range(K):
                    hit = equal_one(rrows[k, source], b)
                    total = total + far[p * K + k] * hit
                return total

            total = lax.fori_loop(0, D, add, total, unroll=8)
            inverse = 1.0 / (1.0 + total[F:])
            at = pl.multiple_of(i * T, T)
            whole_at = pl.multiple_of(b * T, T)
            inv[:, pl.ds(whole_at, T)] = inverse
            xa[ch, c, :, pl.ds(at, T)] = (total[:F] * inverse[:1]).astype(BF16)
            return carry

        lax.fori_loop(0, CB, place, 0)
        copy = rcopy(xa.at[ch, c], xa.at[ch, c], xa_s.at[ch], xa_r.at[ch], d, mate)
        copy.start()
        agg_copies.append(copy)

    for copy in weight_copies:
        copy.wait_recv()
    for i, ref in enumerate((wts, wtn)):
        block = ref[...].reshape(R * F, 2 * F)
        turned = block.astype(F32).T.astype(BF16)
        wb[i] = turned.reshape(2, F, R * F)
    lefts = []
    for q in range(G):
        t = cross(q)
        lefts.append(jnp.concatenate([wts[t], wtn[t]], axis=1))
    left = jnp.concatenate(lefts, axis=0)
    feat_copy.wait_recv()

    def stacked(ch):
        near_part = xf[:, :, ch * CH : (ch + 1) * CH].reshape(2 * F, CH)
        return jnp.concatenate([near_part, xa[ch].reshape(2 * F, CH)], axis=0)

    part_copies = []
    for ch in range(CHUNKS):
        agg_copies[ch].wait_recv()
        part = mm(left, stacked(ch))
        for q in range(1, G):
            psend[q, ch] = part[q * F : (q + 1) * F].astype(BF16)
            copy = rcopy(
                psend.at[q, ch],
                precv.at[q, ch],
                pp_s.at[q, ch],
                pp_r.at[q, ch],
                d,
                cross(q),
            )
            copy.start()
            part_copies.append(copy)
        own[ch] = part[:F]

    loads[2].wait()
    cross_copies, mate_copies = [], []
    for ch in range(CHUNKS):
        preact = own[ch]
        for q in range(1, G):
            part_copies[ch * (G - 1) + q - 1].wait_recv()
            preact = preact + precv[q, ch].astype(F32)
        s = jax.nn.sigmoid(preact)
        at = slice(ch * CH, (ch + 1) * CH)
        out_o[:, at] = (preact * s).astype(BF16)
        slope = s * (1.0 + preact * (1.0 - s))
        gp[ch, r] = (cot[:, at].astype(F32) * slope).astype(BF16)
        for q in range(1, G):
            copy = rcopy(
                gp.at[ch, r],
                gp.at[ch, r],
                gx_s.at[q, ch],
                gx_r.at[q, ch],
                d,
                cross(q),
            )
            copy.start()
            cross_copies.append(copy)
        copy = rcopy(
            gp.at[ch, r], gp.at[ch, r], gc_s.at[0, ch], gc_r.at[0, ch], d, mate
        )
        copy.start()
        mate_copies.append(copy)

    back_left = jnp.concatenate([wb[0, c], wb[1, c]], axis=0)

    def back_chunk(ch):
        later = CHUNKS + ch * (G - 1)
        for copy in [mate_copies[ch]] + mate_copies[later : later + G - 1]:
            copy.wait_recv()
        back = mm(back_left, gp[ch].reshape(R * F, CH))
        for i in range(CB):
            b = ch * CB + i
            at = slice(i * T, (i + 1) * T)
            whole_at = slice(b * T, (b + 1) * T)
            acc_o[:, whole_at] = back[:F, at]
            scaled[b] = (back[F:, at] * inv[:1, whole_at]).astype(BF16)

    def scatter_all():
        def near_back(b, carry):
            right = jnp.concatenate([ltiles[b, l] for l in range(L)], axis=1)
            both = mm(scaled[b], right)
            for l in range(L):
                nearb[l, b] = both[:, l * T : (l + 1) * T]
            return carry

        lax.fori_loop(0, B, near_back, 0, unroll=4)

        def gather_back(block, carry):
            at = pl.ds(pl.multiple_of(block * T, T), T)

            def add(i, total):
                for l in range(L):
                    total = total + nearb[l, i] * equal_one(cols[l, i], block)
                return total

            acc_o[:, at] = lax.fori_loop(0, B, add, acc_o[:, at], unroll=8)
            return carry

        lax.fori_loop(0, B, gather_back, 0)

    grads = jnp.zeros((G * F, 4 * F), F32)
    for ch in range(CHUNKS):
        blocks = [gp[ch, r]]
        for q in range(1, G):
            cross_copies[ch * (G - 1) + q - 1].wait_recv()
            t = lax.rem(g - q + G, G) * 2 + c
            copy = rcopy(
                gp.at[ch, t], gp.at[ch, t], gc_s.at[q, ch], gc_r.at[q, ch], d, mate
            )
            copy.start()
            mate_copies.append(copy)
        for q in range(1, G):
            blocks.append(gp[ch, cross(q)])
        grads = grads + mm_nt(jnp.concatenate(blocks, axis=0), stacked(ch))
        if ch >= 1:
            back_chunk(ch - 1)
    rows = gw.shape[2]
    for p in range(D):
        for q in range(G):
            gw[p, q] = grads[q * F + p * rows : q * F + (p + 1) * rows]

    def piece(p):
        to = lax.rem(d + p, D)
        return rcopy(gw.at[to], gpart.at[p], p_s.at[p], p_r.at[p], to, r)

    def send_piece(p, carry):
        piece(p).start()
        return carry

    lax.fori_loop(1, D, send_piece, 0)

    back_chunk(CHUNKS - 1)

    def away(p, dst, slot):
        source = lax.rem(d + p, D)
        for k in range(K):
            block = scaled[rrows[k, source]]
            dst[slot, k] = mm(block, rtiles[source, k]).astype(BF16)

    def returned(p):
        to = lax.rem(d + p, D)
        return rcopy(ret.at[p], back_o.at[d], b_s.at[p], b_r.at[p], to, r)

    def send_back(p, carry):
        away(p, ret, p)
        returned(p).start()
        return carry

    lax.fori_loop(1, D, send_back, 0, unroll=7)
    away(0, back_o, d)

    def take_piece(p, total):
        piece(p).wait_recv()
        return total + gpart[p]

    red[...] = lax.fori_loop(1, D, take_piece, gw[d])
    finals = []
    for q in range(G):
        for p in range(D):
            if p or q:
                copy = rcopy(
                    red.at[q],
                    final_o.at[g, d],
                    f_s.at[q, p],
                    f_r.at[q, p],
                    lax.rem(d + p, D),
                    cross(q),
                )
                copy.start()
                finals.append(copy)
    final_o[g, d] = red[0]

    scatter_all()

    def finish_back(p, carry):
        returned(p).wait()
        piece(p).wait_send()
        return carry

    lax.fori_loop(1, D, finish_back, 0)
    for copy in finals:
        copy.wait_recv()

    def drain(p, carry):
        halo(p).wait_send()
        return carry

    lax.fori_loop(1, D, drain, 0)
    for copy in (
        weight_copies
        + cross_weights
        + [feat_copy]
        + agg_copies
        + part_copies
        + cross_copies
        + mate_copies
        + finals
    ):
        copy.wait_send()


def finish_kernel(
    slist, acc_h, back_h, final_h, out_h, out_o, gf_o, gs_o, gn_o, total, back, final, sem
):
    F, N = acc_h.shape
    loads = [
        pltpu.make_async_copy(src, dst, sem.at[i])
        for i, (src, dst) in enumerate(
            ((out_h, out_o), (acc_h, total), (back_h, back), (final_h, final))
        )
    ]
    for load in loads:
        load.start()
    D, K, _, T = back.shape
    G, _, rows, width = final.shape
    half = width // 2
    for load in loads[1:]:
        load.wait()

    def home(s, carry):
        for k in range(K):
            at = pl.ds(pl.multiple_of(slist[k, s] * T, T), T)
            total[:, at] = total[:, at] + back[s, k].astype(F32)
        return carry

    lax.fori_loop(0, D, home, 0)
    gf_o[...] = total[...].astype(BF16)
    for h in range(G):
        at = slice(h * half, (h + 1) * half)
        for p in range(D):
            part = final[h, p]
            where = slice(p * rows, (p + 1) * rows)
            gs_o[where, at] = part[:, :half]
            gn_o[where, at] = part[:, half:]
    loads[0].wait()


def local(
    D,
    R,
    feats,
    w_self,
    w_neigh,
    local_cols,
    local_tiles,
    send_list,
    remote_rows,
    remote_tiles,
    cotangent,
):
    F, N = feats.shape
    B, L, T, _ = local_tiles.shape
    K = send_list.shape[2]
    G = R // 2
    CH = N // CHUNKS
    rows = F // D
    vmem = pl.BlockSpec(memory_space=pltpu.VMEM)
    smem = pl.BlockSpec(memory_space=pltpu.SMEM)
    hbm = pl.BlockSpec(memory_space=pl.ANY)
    dma = pltpu.SemaphoreType.DMA
    slist = jnp.swapaxes(send_list, 1, 2)[0]
    rrows = jnp.swapaxes(remote_rows, 1, 2)[0]
    far_tiles = remote_tiles[0]
    limit = 60 * 1024 * 1024
    output, acc, back, final = pl.pallas_call(
        functools.partial(main_kernel, D, R),
        out_shape=(
            jax.ShapeDtypeStruct((F, N), BF16),
            jax.ShapeDtypeStruct((F, N), F32),
            jax.ShapeDtypeStruct((D, K, F, T), BF16),
            jax.ShapeDtypeStruct((G, D, rows, 4 * F), F32),
        ),
        in_specs=[vmem, vmem, vmem, smem, smem, smem, hbm, hbm, hbm],
        out_specs=(vmem, vmem, vmem, vmem),
        scratch_shapes=[
            pltpu.VMEM((B, L, T, T), BF16),
            pltpu.VMEM((D, K, T, T), BF16),
            pltpu.VMEM((F, N), BF16),
            pltpu.VMEM((B, F, T), BF16),
            pltpu.VMEM((D, K, F, T), BF16),
            pltpu.VMEM((D, K, F, T), BF16),
            pltpu.VMEM((B, F + KEEP, T), F32),
            pltpu.VMEM((D * K, F + KEEP, T), F32),
            pltpu.VMEM((KEEP, N), F32),
            pltpu.VMEM((R, F, 2 * F), BF16),
            pltpu.VMEM((R, F, 2 * F), BF16),
            pltpu.VMEM((2, 2, F, R * F), BF16),
            pltpu.VMEM((2, F, N), BF16),
            pltpu.VMEM((CHUNKS, 2, F, CH), BF16),
            pltpu.VMEM((CHUNKS, F, CH), F32),
            pltpu.VMEM((G, CHUNKS, F, CH), BF16),
            pltpu.VMEM((G, CHUNKS, F, CH), BF16),
            pltpu.VMEM((CHUNKS, R, F, CH), BF16),
            pltpu.VMEM((D, G, rows, 4 * F), F32),
            pltpu.VMEM((D, G, rows, 4 * F), F32),
            pltpu.VMEM((G, rows, 4 * F), F32),
            pltpu.VMEM((B, F, T), BF16),
            pltpu.VMEM((D, K, F, T), BF16),
            pltpu.VMEM((L, B, F, T), F32),
            dma((3,)),
            dma((D,)),
            dma((D,)),
            dma((R,)),
            dma((R,)),
            dma((R,)),
            dma((R,)),
            dma,
            dma,
            dma((CHUNKS,)),
            dma((CHUNKS,)),
            dma((G, CHUNKS)),
            dma((G, CHUNKS)),
            dma((G, CHUNKS)),
            dma((G, CHUNKS)),
            dma((G, CHUNKS)),
            dma((G, CHUNKS)),
            dma((D,)),
            dma((D,)),
            dma((D,)),
            dma((D,)),
            dma((G, D)),
            dma((G, D)),
        ],
        compiler_params=pltpu.CompilerParams(
            collective_id=0, has_side_effects=True, vmem_limit_bytes=limit
        ),
        name="layer_main",
    )(
        feats,
        w_self.T,
        w_neigh.T,
        local_cols.T,
        slist,
        rrows,
        local_tiles,
        far_tiles,
        cotangent,
    )
    output, grad_feats, gs, gn = pl.pallas_call(
        finish_kernel,
        out_shape=(
            jax.ShapeDtypeStruct((F, N), BF16),
            jax.ShapeDtypeStruct((F, N), BF16),
            jax.ShapeDtypeStruct((F, R * F), F32),
            jax.ShapeDtypeStruct((F, R * F), F32),
        ),
        in_specs=[smem, hbm, hbm, hbm, hbm],
        out_specs=(vmem, vmem, vmem, vmem),
        scratch_shapes=[
            pltpu.VMEM((F, N), F32),
            pltpu.VMEM((D, K, F, T), BF16),
            pltpu.VMEM((G, D, rows, 4 * F), F32),
            dma((4,)),
        ],
        compiler_params=pltpu.CompilerParams(vmem_limit_bytes=limit),
        name="finish",
    )(slist, acc, back, final, output)
    return output, grad_feats, gs.T, gn.T


def solution(mesh):
    placed = (
        P("rep", "dom"),
        P(None, "rep"),
        P(None, "rep"),
        P("dom", None),
        P("dom", None, None, None),
        P("dom", None, None),
        P("dom", None, None),
        P("dom", None, None, None, None),
        P("rep", "dom"),
    )
    return jax.shard_map(
        functools.partial(local, mesh.shape["dom"], mesh.shape["rep"]),
        mesh=mesh,
        in_specs=placed,
        out_specs=(P("rep", "dom"), P("rep", "dom"), P(None, "rep"), P(None, "rep")),
        check_vma=False,
    )
```

profile of v0, /device:TPU:0, one launch (start us, length us, event | category | flops | bytes accessed | tf_op | source)
XLA Modules:
  0.0 62.4 jit_solution(1152844338692277384)
XLA Ops:
  0.6 58.4 %layer_main.1 = (bf16[64,4096]{1,0:T(8,128)(2,1)}, f32[64,4096]{1,0:T(8,128)}, bf16[8,2,64,128]{3,2,1,0:T(8,128)(2,1)}, f32[2,8,8,256]{3,2,1,0:T(8,128)}) custom-call(bf16[64,4096]{1,0:T(8,128)(2,1)} %feats.1, bf16[64,256]{1,0:T(8,128)(2,1)} %bitcast.13, bf16[64,256]{1,0:T(8,128)(2,1)} %bitcast.14, s32[2,32]{1,0:T(2,128)} %bitcast.17, s32[2,8]{1,0:T(2,128)} %bitcast.15, ...), custom_call_target="tpu_custom_call" | custom-call | tf_op jit(solution)/shard_map/layer_main/pallas_call | solution.py:522
  59.0 3.4 %finish.1 = (bf16[64,4096]{1,0:T(8,128)(2,1)}, bf16[64,4096]{1,0:T(8,128)(2,1)}, f32[64,256]{1,0:T(8,128)}, f32[64,256]{1,0:T(8,128)}) custom-call(s32[2,8]{1,0:T(2,128)} %bitcast.16, f32[64,4096]{1,0:T(8,128)} %get-tuple-element.12.acc_h, bf16[8,2,64,128]{3,2,1,0:T(8,128)(2,1)} %get-tuple-element.13.back_h, f32[2,8,8,256]{3,2,1,0:T(8,128)} %get-tuple-element.14.final_h, ...), custom_call_target="tpu_custom_call" | custom-call | tf_op jit(solution)/shard_map/finish/pallas_call | solution.py:596
where the time goes:
time: 62.6 us; the launch traced here: 62.4 us
  Pallas kernels  61.7 us (99%)
  between operations  0.64 us (1%)
    pallas_call x1, Pallas kernels, local(): pl.pallas_call(functools.partial(main_kernel, D, R), out_shape=(jax.Shape...  58.4 us
    pallas_call x1, Pallas kernels, local(): pl.pallas_call(finish_kernel, out_shape=(jax.ShapeDtypeStruct((F, N), BF1...  3.37 us

commit v1 on v0

--- a/solution.py
+++ b/solution.py
@@ -457,22 +457,14 @@
 
 
 def finish_kernel(
-    slist, acc_h, back_h, final_h, out_h, out_o, gf_o, gs_o, gn_o, total, back, final, sem
+    slist, acc, back, final, out_v, out_o, gf_o, gs_o, gn_o, total, sem
 ):
-    F, N = acc_h.shape
-    loads = [
-        pltpu.make_async_copy(src, dst, sem.at[i])
-        for i, (src, dst) in enumerate(
-            ((out_h, out_o), (acc_h, total), (back_h, back), (final_h, final))
-        )
-    ]
-    for load in loads:
-        load.start()
+    store = pltpu.make_async_copy(out_v, out_o, sem)
+    store.start()
+    total[...] = acc[...]
     D, K, _, T = back.shape
     G, _, rows, width = final.shape
     half = width // 2
-    for load in loads[1:]:
-        load.wait()
 
     def home(s, carry):
         for k in range(K):
@@ -489,7 +481,7 @@
             where = slice(p * rows, (p + 1) * rows)
             gs_o[where, at] = part[:, :half]
             gn_o[where, at] = part[:, half:]
-    loads[0].wait()
+    store.wait()
 
 
 def local(
@@ -513,19 +505,19 @@
     rows = F // D
     vmem = pl.BlockSpec(memory_space=pltpu.VMEM)
     smem = pl.BlockSpec(memory_space=pltpu.SMEM)
-    hbm = pl.BlockSpec(memory_space=pl.ANY)
+    hbm = pl.BlockSpec(memory_space=pltpu.HBM)
     dma = pltpu.SemaphoreType.DMA
     slist = jnp.swapaxes(send_list, 1, 2)[0]
     rrows = jnp.swapaxes(remote_rows, 1, 2)[0]
     far_tiles = remote_tiles[0]
-    limit = 60 * 1024 * 1024
+    limit = 56 * 1024 * 1024
     output, acc, back, final = pl.pallas_call(
         functools.partial(main_kernel, D, R),
         out_shape=(
-            jax.ShapeDtypeStruct((F, N), BF16),
-            jax.ShapeDtypeStruct((F, N), F32),
-            jax.ShapeDtypeStruct((D, K, F, T), BF16),
-            jax.ShapeDtypeStruct((G, D, rows, 4 * F), F32),
+            pltpu.VMEM((F, N), BF16),
+            pltpu.VMEM((F, N), F32),
+            pltpu.VMEM((D, K, F, T), BF16),
+            pltpu.VMEM((G, D, rows, 4 * F), F32),
         ),
         in_specs=[vmem, vmem, vmem, smem, smem, smem, hbm, hbm, hbm],
         out_specs=(vmem, vmem, vmem, vmem),
@@ -601,15 +593,10 @@
             jax.ShapeDtypeStruct((F, R * F), F32),
             jax.ShapeDtypeStruct((F, R * F), F32),
         ),
-        in_specs=[smem, hbm, hbm, hbm, hbm],
-        out_specs=(vmem, vmem, vmem, vmem),
-        scratch_shapes=[
-            pltpu.VMEM((F, N), F32),
-            pltpu.VMEM((D, K, F, T), BF16),
-            pltpu.VMEM((G, D, rows, 4 * F), F32),
-            dma((4,)),
-        ],
-        compiler_params=pltpu.CompilerParams(vmem_limit_bytes=limit),
+        in_specs=[smem, vmem, vmem, vmem, vmem],
+        out_specs=(hbm, vmem, vmem, vmem),
+        scratch_shapes=[pltpu.VMEM((F, N), F32), dma],
+        compiler_params=pltpu.CompilerParams(vmem_limit_bytes=24 * 1024 * 1024),
         name="finish",
     )(slist, acc, back, final, output)
     return output, grad_feats, gs.T, gn.T

time: 62.6 us -> 60.1 us (0.960)
  Pallas kernels: 61.7 us -> 59.3 us
    pallas_call x1, Pallas kernels: 58.4 us -> 57.1 us  [local(): pl.pallas_call(functools.partial(main_kernel, D, R), out_shape=(pltpu.VME...]
    pallas_call x1, Pallas kernels: 3.37 us -> 2.17 us  [local(): pl.pallas_call(finish_kernel, out_shape=(jax.ShapeDtypeStruct((F, N), BF1...]
where the time goes in v1:
time: 60.1 us; the launch traced here: 59.9 us
  Pallas kernels  59.3 us (99%)
  between operations  0.66 us (1%)
    pallas_call x1, Pallas kernels, local(): pl.pallas_call(functools.partial(main_kernel, D, R), out_shape=(pltpu.VME...  57.1 us
    pallas_call x1, Pallas kernels, local(): pl.pallas_call(finish_kernel, out_shape=(jax.ShapeDtypeStruct((F, N), BF1...  2.17 us

profile of v1, /device:TPU:0, one launch (start us, length us, event | category | flops | bytes accessed | tf_op | source)
XLA Modules:
  0.0 59.9 jit_solution(14176136038494857035)
XLA Ops:
  0.6 0.0 copy-start
  0.6 57.1 %layer_main.1 = (bf16[64,4096]{1,0:T(8,128)(2,1)S(1)}, f32[64,4096]{1,0:T(8,128)S(1)}, bf16[8,2,64,128]{3,2,1,0:T(8,128)(2,1)S(1)}, f32[2,8,8,256]{3,2,1,0:T(8,128)S(1)}) custom-call(bf16[64,4096]{1,0:T(8,128)(2,1)} %feats.1, bf16[64,256]{1,0:T(8,128)(2,1)} %bitcast.15, bf16[64,256]{1,0:T(8,128)(2,1)} %bitcast.16, s32[2,32]{1,0:T(2,128)} %bitcast.17, ...), custom_call_target="tpu_custom_call" | custom-call | tf_op jit(solution)/shard_map/layer_main/pallas_call | solution.py:514
  57.7 0.0 copy-done
  57.8 2.2 %finish.1 = (bf16[64,4096]{1,0:T(8,128)(2,1)}, bf16[64,4096]{1,0:T(8,128)(2,1)}, f32[64,256]{1,0:T(8,128)}, f32[64,256]{1,0:T(8,128)}) custom-call(s32[2,8]{1,0:T(2,128)S(1)} %bitcast.13, f32[64,4096]{1,0:T(8,128)S(1)} %get-tuple-element.12.acc, bf16[8,2,64,128]{3,2,1,0:T(8,128)(2,1)S(1)} %get-tuple-element.13.back, ...), custom_call_target="tpu_custom_call" | custom-call | tf_op jit(solution)/shard_map/finish/pallas_call | solution.py:588
Async XLA Ops:
  0.6 57.1 %copy-start = (s32[1,8,2]{1,2,0:T(2,128)S(1)}, s32[1,8,2]{1,2,0:T(2,128)}, u32[]{:S(2)}) copy-start(s32[1,8,2]{1,2,0:T(2,128)} %param.14) | copy-start | bytes 196

commit v2 on v1

v2 whole, which is shorter than its diff:
```python
import functools

import jax
import jax.numpy as jnp
from jax import lax
from jax.experimental import pallas as pl
from jax.experimental.pallas import tpu as pltpu
from jax.sharding import PartitionSpec as P

MESH = pl.DeviceIdType.MESH
F32 = jnp.float32
BF16 = jnp.bfloat16
CHUNKS = 4
PIECES = 4
ONES = 16
KEEP = 8
NT = (((1,), (1,)), ((), ()))


def mm(a, b):
    return jnp.dot(a, b, preferred_element_type=F32)


def mm_nt(a, b):
    return lax.dot_general(a, b, NT, preferred_element_type=F32)


def equal_int(x, y):
    gap = x - y
    return 1 - jnp.minimum(gap * gap, 1)


def equal_one(x, y):
    return equal_int(x, y).astype(F32)


def rcopy(src, dst, send, recv, dom, rep):
    return pltpu.make_async_remote_copy(
        src_ref=src,
        dst_ref=dst,
        send_sem=send,
        recv_sem=recv,
        device_id={"dom": dom, "rep": rep},
        device_id_type=MESH,
    )


def main_kernel(
    D,
    R,
    feats_h,
    wts_h,
    wtn_h,
    cols,
    slist,
    rrows,
    ltiles_h,
    rtiles_h,
    cot_h,
    out_o,
    acc_o,
    back_o,
    final_o,
    fown,
    fmir,
    xchip,
    xmir,
    ltiles,
    rtiles,
    wall,
    wl,
    wb,
    cotb,
    hsend,
    hx,
    sums,
    chain,
    inv,
    xa,
    pre,
    gpb,
    outm,
    accm,
    scaled,
    scm,
    gmate,
    gin,
    gw,
    gpart,
    red,
    ret,
    nearb,
    prev,
    last,
    f_l,
    own_l,
    mir_l,
    w_l,
    c_l,
    t_l,
    xs_s,
    xs_r,
    xm_s,
    xm_r,
    xf_s,
    xf_r,
    h_s,
    h_r,
    hf_s,
    hf_r,
    w_s,
    w_r,
    cm_s,
    cm_r,
    cx_s,
    cx_r,
    om_s,
    om_r,
    am_s,
    am_r,
    sm_s,
    sm_r,
    gm_s,
    gm_r,
    b_s,
    b_r,
    p_s,
    p_r,
    f_s,
    f_r,
):
    d, r = lax.axis_index("dom"), lax.axis_index("rep")
    G = R // 2
    c, g = lax.rem(r, 2), lax.div(r, 2)
    mate = g * 2 + 1 - c
    F, N = feats_h.shape
    B, L, T, _ = ltiles.shape
    K = slist.shape[0]
    RF, CF, S = R * F, 2 * F, D * K
    BH, NH = B // 2, N // 2
    CB = BH // CHUNKS
    CH = CB * T
    PB = B // PIECES
    chips = [lax.rem(g + q, G) for q in range(G)]

    def peer(q, core):
        return chips[q] * 2 + core

    def ahead(p):
        return lax.rem(d + p, D)

    barrier = pltpu.get_barrier_semaphore()
    greeted = [(ahead(p), r) for p in range(1, D)] + [(d, mate)]
    greeted += [(d, peer(q, core)) for q in range(1, G) for core in range(2)]
    for dom, rep in greeted:
        pl.semaphore_signal(
            barrier, inc=1, device_id={"dom": dom, "rep": rep}, device_id_type=MESH
        )
    feat_loads = [
        pltpu.make_async_copy(
            feats_h.at[:, b * T : (b + 1) * T], fown.at[b], f_l.at[b]
        )
        for b in range(B)
    ]
    weight_loads = [
        pltpu.make_async_copy(src, wall.at[r, i], w_l.at[i])
        for i, src in enumerate((wts_h, wtn_h))
    ]

    def half_cut(core, ch):
        return pl.ds(pl.multiple_of(core * NH + ch * CH, T), CH)

    cot_loads = [
        pltpu.make_async_copy(cot_h.at[:, half_cut(c, ch)], cotb.at[ch, r], c_l.at[ch])
        for ch in range(CHUNKS)
    ]
    tile_loads = [
        pltpu.make_async_copy(ltiles_h, ltiles, t_l.at[0]),
        pltpu.make_async_copy(rtiles_h, rtiles, t_l.at[1]),
    ]
    for load in feat_loads + weight_loads + tile_loads + cot_loads:
        load.start()

    def previous(s, carry):
        row = rrows[lax.rem(s, K), lax.rem(d - lax.div(s, K) + D, D)]

        def look(j, found):
            other = rrows[lax.rem(j, K), lax.rem(d - lax.div(j, K) + D, D)]
            return jnp.maximum(found, (j + 1) * equal_int(row, other))

        prev[s] = lax.fori_loop(0, s, look, 0)
        return carry

    lax.fori_loop(0, S, previous, 0)

    def latest(i, carry):
        def look(j, found):
            other = rrows[lax.rem(j, K), lax.rem(d - lax.div(j, K) + D, D)]
            return jnp.maximum(found, (j + 1) * equal_int(c * BH + i, other))

        last[i] = lax.fori_loop(0, S, look, 0)
        return carry

    lax.fori_loop(0, BH, latest, 0)
    for q in range(G):
        chain[q, 0] = jnp.zeros((CF + KEEP, T), F32)
    for load in feat_loads:
        load.wait()
    pl.semaphore_wait(barrier, len(greeted))

    sends = []

    def go(copy):
        copy.start()
        sends.append(copy)
        return copy

    def piece_cut(j):
        return pl.ds(j * PB, PB)

    cross_feats = [
        [
            go(
                rcopy(
                    fown.at[piece_cut(j)],
                    fmir.at[G - q - 1, piece_cut(j)],
                    xs_s.at[q, j],
                    xs_r.at[G - q, j],
                    d,
                    peer(q, c),
                )
            )
            for q in range(1, G)
        ]
        for j in range(PIECES)
    ]
    mate_feat = go(rcopy(fown, xchip.at[c], xm_s, xm_r, d, mate))

    def halo(q, p):
        return rcopy(
            hsend.at[q, p], hx.at[q, c, p], h_s.at[q, p], h_r.at[q, p], ahead(p), r
        )

    def halo_on(q, p):
        return rcopy(
            hx.at[q, c, p], hx.at[q, c, p], hf_s.at[q, p], hf_r.at[q, p], d, mate
        )

    def send_halo(p, carry):
        for k in range(K):
            hsend[0, p, k] = fown[slist[k, ahead(p)]]
        halo(0, p).start()
        return carry

    lax.fori_loop(1, D, send_halo, 0)
    own_copy = pltpu.make_async_copy(fown, xchip.at[c], own_l)
    own_copy.start()
    for load in weight_loads:
        load.wait()
    mate_weights = go(rcopy(wall.at[r], wall.at[r], w_s.at[0], w_r.at[0], d, mate))
    cross_weights = [
        go(rcopy(wall.at[r], wall.at[r], w_s.at[q], w_r.at[q], d, peer(q, c)))
        for q in range(1, G)
    ]
    mate_cots = []
    for ch in range(CHUNKS):
        for q in range(1, G):
            for core in range(2):
                go(
                    rcopy(
                        cot_h.at[:, half_cut(core, ch)],
                        cotb.at[ch, r],
                        cx_s.at[q, core, ch],
                        cx_r.at[q, c, ch],
                        d,
                        peer(q, core),
                    )
                )
        mate_cots.append(
            go(
                rcopy(
                    cot_h.at[:, half_cut(1 - c, ch)],
                    cotb.at[ch, r],
                    cm_s.at[ch],
                    cm_r.at[ch],
                    d,
                    mate,
                )
            )
        )

    def wait_cot(ch):
        cot_loads[ch].wait()
        mate_cots[ch].wait_recv()
        for q in range(1, G):
            for core in range(2):
                slot = cotb.at[ch, r]
                copy = rcopy(
                    slot, slot, cx_s.at[q, core, ch], cx_r.at[q, core, ch], d, mate
                )
                copy.wait_recv()

    ones = jnp.ones((ONES, T), BF16)
    ones_wide = jnp.ones((ONES, L * T), BF16)

    def near(q, x):
        def step(i, carry):
            b = c * BH + i
            left = jnp.concatenate(
                [
                    jnp.concatenate([x(core, cols[l, b]) for core in range(2)], axis=0)
                    for l in range(L)
                ],
                axis=1,
            )
            if q == 0:
                left = jnp.concatenate([left, ones_wide], axis=0)
            right = jnp.concatenate([ltiles[b, l] for l in range(L)], axis=1)
            high = CF + KEEP if q == 0 else CF
            sums[q, i, :high] = mm_nt(left, right)[:high]
            return carry

        lax.fori_loop(0, BH, step, 0, unroll=4)

    def far(q):
        def step(p, carry):
            source = lax.rem(d - p + D, D)
            high = CF + KEEP if q == 0 else CF
            for k in range(K):
                s = p * K + k
                left = [hx[q, core, p, k] for core in range(2)]
                if q == 0:
                    left.append(ones)
                term = mm_nt(jnp.concatenate(left, axis=0), rtiles[source, k])[:high]
                chain[q, s + 1, :high] = term + chain[q, prev[s], :high]
            return carry

        lax.fori_loop(0, D, step, 0, unroll=4)

    def place(q):
        def step(i, carry):
            if q == 0:
                total = sums[q, i] + chain[q, last[i]]
                inverse = 1.0 / (1.0 + total[CF:])
                inv[i] = inverse
            else:
                total = sums[q, i, :CF] + chain[q, last[i], :CF]
                inverse = inv[i]
            xa[q, i] = (total[:CF] * inverse[:1]).astype(BF16)
            return carry

        lax.fori_loop(0, BH, step, 0, unroll=4)

    feats_on = []

    def pass_feats(j):
        for q in range(1, G):
            cross_feats[j][G - q - 1].wait_recv()
            feats_on.append(
                go(
                    rcopy(
                        fmir.at[q - 1, piece_cut(j)],
                        xmir.at[q - 1, c, piece_cut(j)],
                        xf_s.at[q, j],
                        xf_r.at[q, j],
                        d,
                        mate,
                    )
                )
            )

    def pass_halo(q):
        def step(p, carry):
            halo(q, p).wait_recv()
            halo_on(q, p).start()
            return carry

        lax.fori_loop(1, D, step, 0)

    def wait_halo(q):
        def step(p, carry):
            halo_on(q, p).wait_recv()
            return carry

        lax.fori_loop(1, D, step, 0)

    own_copy.wait()
    mate_feat.wait_recv()
    for k in range(K):
        for core in range(2):
            hx[0, core, 0, k] = xchip[core, slist[k, d]]
    tile_loads[0].wait()
    near(0, lambda core, col: xchip[core, col])
    tile_loads[1].wait()
    pass_feats(0)
    pass_halo(0)
    for j in range(1, PIECES - 1):
        pass_feats(j)
    wait_halo(0)
    far(0)
    place(0)
    pass_feats(PIECES - 1)
    mirror_copies = [
        pltpu.make_async_copy(fmir.at[q - 1], xmir.at[q - 1, c], mir_l.at[q - 1])
        for q in range(1, G)
    ]

    for q in range(1, G):

        def send_mirror(p, carry):
            for k in range(K):
                hsend[q, p, k] = fmir[q - 1, slist[k, ahead(p)]]
            halo(q, p).start()
            return carry

        lax.fori_loop(1, D, send_mirror, 0)
    for copy in mirror_copies:
        copy.start()
    weights_on = []
    for q in range(1, G):
        t = lax.rem(g - q + G, G) * 2 + c
        cross_weights[q - 1].wait_recv()
        slot = G + q - 1
        weights_on.append(
            go(rcopy(wall.at[t], wall.at[t], w_s.at[slot], w_r.at[slot], d, mate))
        )
    mate_weights.wait_recv()
    for copy in weights_on:
        copy.wait_recv()
    order = [r, mate] + [
        rep for q in range(1, G) for rep in (peer(q, c), peer(q, 1 - c))
    ]
    for i in range(2):
        for n, t in enumerate(order):
            for q in range(G):
                cut = pl.ds(pl.multiple_of(chips[q] * CF, CF), CF)
                wl[i, n * F : (n + 1) * F, q * CF : (q + 1) * CF] = wall[t, i, :, cut]
        turned = wl[i, :, :CF].astype(F32).T.astype(BF16)
        wb[i] = turned.reshape(2, F, RF)
    for copy in mirror_copies:
        copy.wait()
    for copy in feats_on:
        copy.wait_recv()
    for q in range(1, G):
        for k in range(K):
            for core in range(2):
                hx[q, core, 0, k] = xmir[q - 1, core, slist[k, d]]
        near(q, lambda core, col: xmir[q - 1, core, col])

    def stacked_x(ch):
        parts = []
        for i in range(CB):
            b = c * BH + ch * CB + i
            rows = [xchip[0, b], xchip[1, b]]
            for q in range(1, G):
                rows += [xmir[q - 1, 0, b], xmir[q - 1, 1, b]]
            parts.append(jnp.concatenate(rows, axis=0))
        return jnp.concatenate(parts, axis=1)

    def stacked_a(ch):
        return jnp.concatenate(
            [
                jnp.concatenate([xa[q, ch * CB + i] for q in range(G)], axis=0)
                for i in range(CB)
            ],
            axis=1,
        )

    for ch in range(CHUNKS):
        pre[ch] = mm(wl[0], stacked_x(ch))
    for q in range(1, G):
        pass_halo(q)
    for q in range(1, G):
        wait_halo(q)
        far(q)
        place(q)

    back_left = jnp.concatenate([wb[0, c], wb[0, 1 - c], wb[1, c], wb[1, 1 - c]], axis=0)
    grads = jnp.zeros((CF, 2 * RF), F32)
    out_copies, acc_copies, scaled_copies = [], [], []
    for ch in range(CHUNKS):
        cut = half_cut(c, ch)
        agg = stacked_a(ch)
        preact = pre[ch] + mm(wl[1], agg)
        s = jax.nn.sigmoid(preact)
        result = (preact[:CF] * s[:CF]).astype(BF16)
        out_o[:, cut] = result[:F]
        outm[ch] = result[F:]
        slope = s * (1.0 + preact * (1.0 - s))
        wait_cot(ch)
        cot = jnp.concatenate([cotb[ch, t] for t in order], axis=0)
        gp = (cot.astype(F32) * slope).astype(BF16)
        gpb[ch] = gp
        back = mm(back_left, gpb[ch])
        at = pl.ds(c * BH + ch * CB, CB)
        for i in range(CB):
            lane = slice(i * T, (i + 1) * T)
            inverse = inv[ch * CB + i][:1]
            scaled[c * BH + ch * CB + i] = (back[CF : CF + F, lane] * inverse).astype(
                BF16
            )
            scm[ch, i] = (back[CF + F :, lane] * inverse).astype(BF16)
        scaled_copies.append(
            go(rcopy(scm.at[ch], scaled.at[at], sm_s.at[ch], sm_r.at[ch], d, mate))
        )
        acc_o[:, cut] = back[:F]
        accm[ch] = back[F:CF]
        acc_copies.append(
            go(rcopy(accm.at[ch], acc_o.at[:, cut], am_s.at[ch], am_r.at[ch], d, mate))
        )
        out_copies.append(
            go(rcopy(outm.at[ch], out_o.at[:, cut], om_s.at[ch], om_r.at[ch], d, mate))
        )
        both = jnp.concatenate([stacked_x(ch), agg], axis=0)
        grads = grads + mm_nt(gpb[ch, :CF], both)
    gmate[...] = grads[F:]
    grad_copy = go(rcopy(gmate, gin, gm_s, gm_r, d, mate))

    for copy in scaled_copies:
        copy.wait_recv()

    def away(p, dst, slot):
        source = ahead(p)
        for k in range(K):
            block = scaled[rrows[k, source]]
            dst[slot, k] = mm(block, rtiles[source, k]).astype(BF16)

    def returned(p):
        return rcopy(ret.at[p], back_o.at[d], b_s.at[p], b_r.at[p], ahead(p), r)

    def send_back(p, carry):
        away(p, ret, p)
        returned(p).start()
        return carry

    lax.fori_loop(1, D, send_back, 0, unroll=7)
    away(0, back_o, d)

    rows = F // D
    grad_copy.wait_recv()
    own = grads[:F] + gin[...]
    for p in range(D):
        for i in range(2):
            for q in range(G):
                to = pl.ds(pl.multiple_of(i * RF + chips[q] * CF, CF), CF)
                lane = slice(i * RF + q * CF, i * RF + (q + 1) * CF)
                gw[p, :, to] = own[p * rows : (p + 1) * rows, lane]

    def piece(p):
        to = ahead(p)
        return rcopy(gw.at[to], gpart.at[p], p_s.at[p], p_r.at[p], to, r)

    def send_piece(p, carry):
        piece(p).start()
        return carry

    lax.fori_loop(1, D, send_piece, 0)

    def near_back(b, carry):
        right = jnp.concatenate([ltiles[b, l] for l in range(L)], axis=1)
        both = mm(scaled[b], right)
        for l in range(L):
            nearb[l, b] = both[:, l * T : (l + 1) * T]
        return carry

    lax.fori_loop(0, B, near_back, 0, unroll=4)
    for copy in acc_copies:
        copy.wait_recv()

    def gather_back(block, carry):
        at = pl.ds(pl.multiple_of(block * T, T), T)

        def add(i, total):
            for l in range(L):
                total = total + nearb[l, i] * equal_one(cols[l, i], block)
            return total

        acc_o[:, at] = lax.fori_loop(0, B, add, acc_o[:, at], unroll=8)
        return carry

    lax.fori_loop(0, BH, gather_back, 0)

    def take_piece(p, total):
        piece(p).wait_recv()
        return total + gpart[p]

    red[...] = lax.fori_loop(1, D, take_piece, gw[d])

    def final(p):
        return rcopy(red, final_o.at[d], f_s.at[p], f_r.at[p], ahead(p), r)

    def send_final(p, carry):
        final(p).start()
        return carry

    lax.fori_loop(1, D, send_final, 0)
    final_o[d] = red[...]
    lax.fori_loop(BH, B, gather_back, 0)
    for copy in out_copies:
        copy.wait_recv()

    def drain(p, carry):
        for q in range(G):
            halo(q, p).wait_send()
            halo_on(q, p).wait_send()
        returned(p).wait()
        piece(p).wait_send()
        final(p).wait()
        return carry

    lax.fori_loop(1, D, drain, 0)
    for copy in sends:
        copy.wait_send()


def finish_kernel(slist, acc, back, final, out_v, out_o, gf_o, gs_o, gn_o, total, sem):
    store = pltpu.make_async_copy(out_v, out_o, sem)
    store.start()
    total[...] = acc[...]
    D, K, _, T = back.shape
    _, rows, width = final.shape
    half = width // 2

    def home(s, carry):
        for k in range(K):
            at = pl.ds(pl.multiple_of(slist[k, s] * T, T), T)
            total[:, at] = total[:, at] + back[s, k].astype(F32)
        return carry

    lax.fori_loop(0, D, home, 0)
    gf_o[...] = total[...].astype(BF16)
    for p in range(D):
        part = final[p]
        where = slice(p * rows, (p + 1) * rows)
        gs_o[where, :] = part[:, :half]
        gn_o[where, :] = part[:, half:]
    store.wait()


def local(
    D,
    R,
    feats,
    w_self,
    w_neigh,
    local_cols,
    local_tiles,
    send_list,
    remote_rows,
    remote_tiles,
    cotangent,
):
    F, N = feats.shape
    B, L, T, _ = local_tiles.shape
    K = send_list.shape[2]
    G = R // 2
    RF, CF, S = R * F, 2 * F, D * K
    BH = B // 2
    CB = BH // CHUNKS
    CH = CB * T
    rows = F // D
    M = max(G - 1, 1)
    vmem = pl.BlockSpec(memory_space=pltpu.VMEM)
    smem = pl.BlockSpec(memory_space=pltpu.SMEM)
    hbm = pl.BlockSpec(memory_space=pltpu.HBM)
    dma = pltpu.SemaphoreType.DMA
    slist = jnp.swapaxes(send_list, 1, 2)[0]
    rrows = jnp.swapaxes(remote_rows, 1, 2)[0]
    far_tiles = remote_tiles[0]
    limit = 56 * 1024 * 1024
    output, acc, back, final = pl.pallas_call(
        functools.partial(main_kernel, D, R),
        out_shape=(
            pltpu.VMEM((F, N), BF16),
            pltpu.VMEM((F, N), F32),
            pltpu.VMEM((D, K, F, T), BF16),
            pltpu.VMEM((D, rows, 2 * RF), F32),
        ),
        in_specs=[hbm, hbm, hbm, smem, smem, smem, hbm, hbm, hbm],
        out_specs=(vmem, vmem, vmem, vmem),
        scratch_shapes=[
            pltpu.VMEM((B, F, T), BF16),
            pltpu.VMEM((M, B, F, T), BF16),
            pltpu.VMEM((2, B, F, T), BF16),
            pltpu.VMEM((M, 2, B, F, T), BF16),
            pltpu.VMEM((B, L, T, T), BF16),
            pltpu.VMEM((D, K, T, T), BF16),
            pltpu.VMEM((R, 2, F, RF), BF16),
            pltpu.VMEM((2, RF, RF), BF16),
            pltpu.VMEM((2, 2, F, RF), BF16),
            pltpu.VMEM((CHUNKS, R, F, CH), BF16),
            pltpu.VMEM((G, D, K, F, T), BF16),
            pltpu.VMEM((G, 2, D, K, F, T), BF16),
            pltpu.VMEM((G, BH, CF + KEEP, T), F32),
            pltpu.VMEM((G, S + 1, CF + KEEP, T), F32),
            pltpu.VMEM((BH, KEEP, T), F32),
            pltpu.VMEM((G, BH, CF, T), BF16),
            pltpu.VMEM((CHUNKS, RF, CH), F32),
            pltpu.VMEM((CHUNKS, RF, CH), BF16),
            pltpu.VMEM((CHUNKS, F, CH), BF16),
            pltpu.VMEM((CHUNKS, F, CH), F32),
            pltpu.VMEM((B, F, T), BF16),
            pltpu.VMEM((CHUNKS, CB, F, T), BF16),
            pltpu.VMEM((F, 2 * RF), F32),
            pltpu.VMEM((F, 2 * RF), F32),
            pltpu.VMEM((D, rows, 2 * RF), F32),
            pltpu.VMEM((D, rows, 2 * RF), F32),
            pltpu.VMEM((rows, 2 * RF), F32),
            pltpu.VMEM((D, K, F, T), BF16),
            pltpu.VMEM((L, B, F, T), F32),
            pltpu.SMEM((S,), jnp.int32),
            pltpu.SMEM((BH,), jnp.int32),
            dma((B,)),
            dma,
            dma((M,)),
            dma((2,)),
            dma((CHUNKS,)),
            dma((2,)),
            dma((G, PIECES)),
            dma((G, PIECES)),
            dma,
            dma,
            dma((G, PIECES)),
            dma((G, PIECES)),
            dma((G, D)),
            dma((G, D)),
            dma((G, D)),
            dma((G, D)),
            dma((R,)),
            dma((R,)),
            dma((CHUNKS,)),
            dma((CHUNKS,)),
            dma((G, 2, CHUNKS)),
            dma((G, 2, CHUNKS)),
            dma((CHUNKS,)),
            dma((CHUNKS,)),
            dma((CHUNKS,)),
            dma((CHUNKS,)),
            dma((CHUNKS,)),
            dma((CHUNKS,)),
            dma,
            dma,
            dma((D,)),
            dma((D,)),
            dma((D,)),
            dma((D,)),
            dma((D,)),
            dma((D,)),
        ],
        compiler_params=pltpu.CompilerParams(
            collective_id=0, has_side_effects=True, vmem_limit_bytes=limit
        ),
        name="layer_main",
    )(
        feats,
        w_self.T,
        w_neigh.T,
        local_cols.T,
        slist,
        rrows,
        local_tiles,
        far_tiles,
        cotangent,
    )
    output, grad_feats, gs, gn = pl.pallas_call(
        finish_kernel,
        out_shape=(
            jax.ShapeDtypeStruct((F, N), BF16),
            jax.ShapeDtypeStruct((F, N), BF16),
            jax.ShapeDtypeStruct((F, RF), F32),
            jax.ShapeDtypeStruct((F, RF), F32),
        ),
        in_specs=[smem, vmem, vmem, vmem, vmem],
        out_specs=(hbm, vmem, vmem, vmem),
        scratch_shapes=[pltpu.VMEM((F, N), F32), dma],
        compiler_params=pltpu.CompilerParams(vmem_limit_bytes=24 * 1024 * 1024),
        name="finish",
    )(slist, acc, back, final, output)
    return output, grad_feats, gs.T, gn.T


def solution(mesh):
    placed = (
        P("rep", "dom"),
        P(None, "rep"),
        P(None, "rep"),
        P("dom", None),
        P("dom", None, None, None),
        P("dom", None, None),
        P("dom", None, None),
        P("dom", None, None, None, None),
        P("rep", "dom"),
    )
    return jax.shard_map(
        functools.partial(local, mesh.shape["dom"], mesh.shape["rep"]),
        mesh=mesh,
        in_specs=placed,
        out_specs=(P("rep", "dom"), P("rep", "dom"), P(None, "rep"), P(None, "rep")),
        check_vma=False,
    )
```

time: 60.1 us -> 58.8 us (0.978)
  Pallas kernels: 59.3 us -> 58 us
    pallas_call x1, Pallas kernels: 57.1 us -> 55.8 us  [local(): pl.pallas_call(functools.partial(main_kernel, D, R), out_shape=(pltpu.VME...]
where the time goes in v2:
time: 58.8 us; the launch traced here: 58.6 us
  Pallas kernels  58 us (99%)
  between operations  0.66 us (1%)
    pallas_call x1, Pallas kernels, local(): pl.pallas_call(functools.partial(main_kernel, D, R), out_shape=(pltpu.VME...  55.8 us
    pallas_call x1, Pallas kernels, local(): pl.pallas_call(finish_kernel, out_shape=(jax.ShapeDtypeStruct((F, N), BF1...  2.17 us

profile of v2, /device:TPU:0, one launch (start us, length us, event | category | flops | bytes accessed | tf_op | source)
XLA Modules:
  0.0 58.6 jit_solution(17346994522074450497)
XLA Ops:
  0.6 0.0 copy-start
  0.6 55.8 %layer_main.1 = (bf16[64,4096]{1,0:T(8,128)(2,1)S(1)}, f32[64,4096]{1,0:T(8,128)S(1)}, bf16[8,2,64,128]{3,2,1,0:T(8,128)(2,1)S(1)}, f32[8,8,512]{2,1,0:T(8,128)S(1)}) custom-call(bf16[64,4096]{1,0:T(8,128)(2,1)} %feats_h.1, bf16[64,256]{1,0:T(8,128)(2,1)} %bitcast.15, bf16[64,256]{1,0:T(8,128)(2,1)} %bitcast.16, s32[2,32]{1,0:T(2,128)} %bitcast.17, ...), custom_call_target="tpu_custom_call" | custom-call | tf_op jit(solution)/shard_map/layer_main/pallas_call | solution.py:671
  56.4 0.0 copy-done
  56.4 2.2 %finish.1 = (bf16[64,4096]{1,0:T(8,128)(2,1)}, bf16[64,4096]{1,0:T(8,128)(2,1)}, f32[64,256]{1,0:T(8,128)}, f32[64,256]{1,0:T(8,128)}) custom-call(s32[2,8]{1,0:T(2,128)S(1)} %bitcast.13, f32[64,4096]{1,0:T(8,128)S(1)} %get-tuple-element.12.acc, bf16[8,2,64,128]{3,2,1,0:T(8,128)(2,1)S(1)} %get-tuple-element.13.back, ...), custom_call_target="tpu_custom_call" | custom-call | tf_op jit(solution)/shard_map/finish/pallas_call | solution.py:765
Async XLA Ops:
  0.6 55.8 %copy-start = (s32[1,8,2]{1,2,0:T(2,128)S(1)}, s32[1,8,2]{1,2,0:T(2,128)}, u32[]{:S(2)}) copy-start(s32[1,8,2]{1,2,0:T(2,128)} %param.14) | copy-start | bytes 196

commit v3 on v2

--- a/solution.py
+++ b/solution.py
@@ -83,6 +83,7 @@
     accm,
     scaled,
     scm,
+    gown,
     gmate,
     gin,
     gw,
@@ -90,6 +91,7 @@
     red,
     ret,
     nearb,
+    rowtab,
     prev,
     last,
     f_l,
@@ -149,6 +151,21 @@
     def ahead(p):
         return lax.rem(d + p, D)
 
+    def half_cut(core, ch):
+        return pl.ds(pl.multiple_of(core * NH + ch * CH, T), CH)
+
+    def piece_cut(j):
+        return pl.ds(j * PB, PB)
+
+    def taken(ref, sem):
+        pltpu.make_async_copy(ref, ref, sem).wait()
+
+    def went(ref, sem):
+        rcopy(ref, ref, sem, sem, d, mate).wait_send()
+
+    def came(ref, sem):
+        rcopy(ref, ref, sem, sem, d, mate).wait_recv()
+
     barrier = pltpu.get_barrier_semaphore()
     greeted = [(ahead(p), r) for p in range(1, D)] + [(d, mate)]
     greeted += [(d, peer(q, core)) for q in range(1, G) for core in range(2)]
@@ -156,149 +173,88 @@
         pl.semaphore_signal(
             barrier, inc=1, device_id={"dom": dom, "rep": rep}, device_id_type=MESH
         )
-    feat_loads = [
-        pltpu.make_async_copy(
-            feats_h.at[:, b * T : (b + 1) * T], fown.at[b], f_l.at[b]
-        )
+    loads = [
+        pltpu.make_async_copy(feats_h.at[:, b * T : (b + 1) * T], fown.at[b], f_l)
         for b in range(B)
     ]
-    weight_loads = [
-        pltpu.make_async_copy(src, wall.at[r, i], w_l.at[i])
+    loads += [
+        pltpu.make_async_copy(src, wall.at[r, i], w_l)
         for i, src in enumerate((wts_h, wtn_h))
-    ]
-
-    def half_cut(core, ch):
-        return pl.ds(pl.multiple_of(core * NH + ch * CH, T), CH)
-
-    cot_loads = [
-        pltpu.make_async_copy(cot_h.at[:, half_cut(c, ch)], cotb.at[ch, r], c_l.at[ch])
-        for ch in range(CHUNKS)
     ]
     tile_loads = [
         pltpu.make_async_copy(ltiles_h, ltiles, t_l.at[0]),
         pltpu.make_async_copy(rtiles_h, rtiles, t_l.at[1]),
     ]
-    for load in feat_loads + weight_loads + tile_loads + cot_loads:
+    loads += tile_loads
+    loads += [
+        pltpu.make_async_copy(cot_h.at[:, half_cut(c, ch)], cotb.at[ch, r], c_l)
+        for ch in range(CHUNKS)
+    ]
+    for load in loads:
         load.start()
-
-    def previous(s, carry):
-        row = rrows[lax.rem(s, K), lax.rem(d - lax.div(s, K) + D, D)]
-
-        def look(j, found):
-            other = rrows[lax.rem(j, K), lax.rem(d - lax.div(j, K) + D, D)]
-            return jnp.maximum(found, (j + 1) * equal_int(row, other))
-
-        prev[s] = lax.fori_loop(0, s, look, 0)
-        return carry
-
-    lax.fori_loop(0, S, previous, 0)
-
-    def latest(i, carry):
-        def look(j, found):
-            other = rrows[lax.rem(j, K), lax.rem(d - lax.div(j, K) + D, D)]
-            return jnp.maximum(found, (j + 1) * equal_int(c * BH + i, other))
-
-        last[i] = lax.fori_loop(0, S, look, 0)
-        return carry
-
-    lax.fori_loop(0, BH, latest, 0)
-    for q in range(G):
-        chain[q, 0] = jnp.zeros((CF + KEEP, T), F32)
-    for load in feat_loads:
-        load.wait()
+    taken(fown, f_l)
     pl.semaphore_wait(barrier, len(greeted))
 
-    sends = []
-
-    def go(copy):
-        copy.start()
-        sends.append(copy)
-        return copy
-
-    def piece_cut(j):
-        return pl.ds(j * PB, PB)
-
-    cross_feats = [
-        [
-            go(
-                rcopy(
-                    fown.at[piece_cut(j)],
-                    fmir.at[G - q - 1, piece_cut(j)],
-                    xs_s.at[q, j],
-                    xs_r.at[G - q, j],
-                    d,
-                    peer(q, c),
-                )
-            )
-            for q in range(1, G)
-        ]
-        for j in range(PIECES)
-    ]
-    mate_feat = go(rcopy(fown, xchip.at[c], xm_s, xm_r, d, mate))
-
-    def halo(q, p):
-        return rcopy(
-            hsend.at[q, p], hx.at[q, c, p], h_s.at[q, p], h_r.at[q, p], ahead(p), r
-        )
-
-    def halo_on(q, p):
-        return rcopy(
-            hx.at[q, c, p], hx.at[q, c, p], hf_s.at[q, p], hf_r.at[q, p], d, mate
-        )
-
-    def send_halo(p, carry):
-        for k in range(K):
-            hsend[0, p, k] = fown[slist[k, ahead(p)]]
-        halo(0, p).start()
-        return carry
-
-    lax.fori_loop(1, D, send_halo, 0)
+    for j in range(PIECES):
+        for q in range(1, G):
+            rcopy(
+                fown.at[piece_cut(j)],
+                fmir.at[G - q - 1, piece_cut(j)],
+                xs_s.at[q - 1],
+                xs_r.at[G - q - 1, j],
+                d,
+                peer(q, c),
+            ).start()
+    mate_feat = rcopy(fown, xchip.at[c], xm_s, xm_r, d, mate)
+    mate_feat.start()
+
+    def send_halos(q, ref):
+        def step(p, carry):
+            to = ahead(p)
+            for k in range(K):
+                hsend[q, p, k] = ref(slist[k, to])
+            rcopy(
+                hsend.at[q, p], hx.at[q, c, p], h_s.at[q], h_r.at[q], to, r
+            ).start()
+            return carry
+
+        lax.fori_loop(1, D, step, 0)
+
+    others = pl.ds(1, D - 1)
+
+    def halo_on(q):
+        part = hx.at[q, c, others]
+        return rcopy(part, part, hf_s.at[q], hf_r.at[q], d, mate)
+
+    def pass_halo(q):
+        came(hx.at[q, c, others], h_r.at[q])
+        halo_on(q).start()
+
+    send_halos(0, lambda block: fown[block])
     own_copy = pltpu.make_async_copy(fown, xchip.at[c], own_l)
     own_copy.start()
-    for load in weight_loads:
-        load.wait()
-    mate_weights = go(rcopy(wall.at[r], wall.at[r], w_s.at[0], w_r.at[0], d, mate))
-    cross_weights = [
-        go(rcopy(wall.at[r], wall.at[r], w_s.at[q], w_r.at[q], d, peer(q, c)))
-        for q in range(1, G)
-    ]
-    mate_cots = []
+    taken(wall.at[r], w_l)
+    weight_copies = [rcopy(wall.at[r], wall.at[r], w_s.at[0], w_r.at[0], d, mate)]
+    for q in range(1, G):
+        weight_copies.append(
+            rcopy(wall.at[r], wall.at[r], w_s.at[q], w_r.at[q], d, peer(q, c))
+        )
+    for copy in weight_copies:
+        copy.start()
     for ch in range(CHUNKS):
         for q in range(1, G):
             for core in range(2):
-                go(
-                    rcopy(
-                        cot_h.at[:, half_cut(core, ch)],
-                        cotb.at[ch, r],
-                        cx_s.at[q, core, ch],
-                        cx_r.at[q, c, ch],
-                        d,
-                        peer(q, core),
-                    )
-                )
-        mate_cots.append(
-            go(
                 rcopy(
-                    cot_h.at[:, half_cut(1 - c, ch)],
+                    cot_h.at[:, half_cut(core, ch)],
                     cotb.at[ch, r],
-                    cm_s.at[ch],
-                    cm_r.at[ch],
+                    cx_s.at[q - 1],
+                    cx_r.at[q - 1, ch],
                     d,
-                    mate,
-                )
-            )
-        )
-
-    def wait_cot(ch):
-        cot_loads[ch].wait()
-        mate_cots[ch].wait_recv()
-        for q in range(1, G):
-            for core in range(2):
-                slot = cotb.at[ch, r]
-                copy = rcopy(
-                    slot, slot, cx_s.at[q, core, ch], cx_r.at[q, core, ch], d, mate
-                )
-                copy.wait_recv()
+                    peer(q, core),
+                ).start()
+        rcopy(
+            cot_h.at[:, half_cut(1 - c, ch)], cotb.at[ch, r], cm_s, cm_r, d, mate
+        ).start()
 
     ones = jnp.ones((ONES, T), BF16)
     ones_wide = jnp.ones((ONES, L * T), BF16)
@@ -351,38 +307,18 @@
 
         lax.fori_loop(0, BH, step, 0, unroll=4)
 
-    feats_on = []
-
     def pass_feats(j):
         for q in range(1, G):
-            cross_feats[j][G - q - 1].wait_recv()
-            feats_on.append(
-                go(
-                    rcopy(
-                        fmir.at[q - 1, piece_cut(j)],
-                        xmir.at[q - 1, c, piece_cut(j)],
-                        xf_s.at[q, j],
-                        xf_r.at[q, j],
-                        d,
-                        mate,
-                    )
-                )
-            )
-
-    def pass_halo(q):
-        def step(p, carry):
-            halo(q, p).wait_recv()
-            halo_on(q, p).start()
-            return carry
-
-        lax.fori_loop(1, D, step, 0)
-
-    def wait_halo(q):
-        def step(p, carry):
-            halo_on(q, p).wait_recv()
-            return carry
-
-        lax.fori_loop(1, D, step, 0)
+            part = fmir.at[q - 1, piece_cut(j)]
+            came(part, xs_r.at[q - 1, j])
+            rcopy(
+                part,
+                xmir.at[q - 1, c, piece_cut(j)],
+                xf_s.at[q - 1],
+                xf_r.at[q - 1],
+                d,
+                mate,
+            ).start()
 
     own_copy.wait()
     mate_feat.wait_recv()
@@ -392,40 +328,62 @@
     tile_loads[0].wait()
     near(0, lambda core, col: xchip[core, col])
     tile_loads[1].wait()
+
+    def list_rows(p, carry):
+        source = lax.rem(d - p + D, D)
+        for k in range(K):
+            rowtab[p * K + k] = rrows[k, source]
+        return carry
+
+    lax.fori_loop(0, D, list_rows, 0)
+
+    def previous(s, carry):
+        row = rowtab[s]
+
+        def look(j, found):
+            before = jnp.minimum(jnp.maximum(s - j, 0), 1)
+            return jnp.maximum(found, (j + 1) * before * equal_int(row, rowtab[j]))
+
+        prev[s] = lax.fori_loop(0, S, look, 0, unroll=16)
+        return carry
+
+    lax.fori_loop(0, S, previous, 0)
+
+    def latest(i, carry):
+        def look(j, found):
+            return jnp.maximum(found, (j + 1) * equal_int(c * BH + i, rowtab[j]))
+
+        last[i] = lax.fori_loop(0, S, look, 0, unroll=16)
+        return carry
+
+    lax.fori_loop(0, BH, latest, 0)
+    for q in range(G):
+        chain[q, 0] = jnp.zeros((CF + KEEP, T), F32)
     pass_feats(0)
     pass_halo(0)
     for j in range(1, PIECES - 1):
         pass_feats(j)
-    wait_halo(0)
+    halo_on(0).wait_recv()
     far(0)
     place(0)
     pass_feats(PIECES - 1)
+    for q in range(1, G):
+        send_halos(q, lambda block: fmir[q - 1, block])
     mirror_copies = [
         pltpu.make_async_copy(fmir.at[q - 1], xmir.at[q - 1, c], mir_l.at[q - 1])
         for q in range(1, G)
     ]
-
-    for q in range(1, G):
-
-        def send_mirror(p, carry):
-            for k in range(K):
-                hsend[q, p, k] = fmir[q - 1, slist[k, ahead(p)]]
-            halo(q, p).start()
-            return carry
-
-        lax.fori_loop(1, D, send_mirror, 0)
     for copy in mirror_copies:
         copy.start()
-    weights_on = []
     for q in range(1, G):
         t = lax.rem(g - q + G, G) * 2 + c
-        cross_weights[q - 1].wait_recv()
+        weight_copies[q].wait_recv()
         slot = G + q - 1
-        weights_on.append(
-            go(rcopy(wall.at[t], wall.at[t], w_s.at[slot], w_r.at[slot], d, mate))
-        )
-    mate_weights.wait_recv()
-    for copy in weights_on:
+        copy = rcopy(wall.at[t], wall.at[t], w_s.at[slot], w_r.at[slot], d, mate)
+        copy.start()
+        weight_copies.append(copy)
+    weight_copies[0].wait_recv()
+    for copy in weight_copies[G:]:
         copy.wait_recv()
     order = [r, mate] + [
         rep for q in range(1, G) for rep in (peer(q, c), peer(q, 1 - c))
@@ -439,8 +397,8 @@
         wb[i] = turned.reshape(2, F, RF)
     for copy in mirror_copies:
         copy.wait()
-    for copy in feats_on:
-        copy.wait_recv()
+    for q in range(1, G):
+        came(xmir.at[q - 1, 1 - c], xf_r.at[q - 1])
     for q in range(1, G):
         for k in range(K):
             for core in range(2):
@@ -471,26 +429,41 @@
     for q in range(1, G):
         pass_halo(q)
     for q in range(1, G):
-        wait_halo(q)
+        halo_on(q).wait_recv()
         far(q)
         place(q)
 
-    back_left = jnp.concatenate([wb[0, c], wb[0, 1 - c], wb[1, c], wb[1, 1 - c]], axis=0)
+    taken(cotb.at[pl.ds(0, CHUNKS), r], c_l)
+    came(cotb.at[pl.ds(0, CHUNKS), mate], cm_r)
     grads = jnp.zeros((CF, 2 * RF), F32)
-    out_copies, acc_copies, scaled_copies = [], [], []
     for ch in range(CHUNKS):
         cut = half_cut(c, ch)
         agg = stacked_a(ch)
         preact = pre[ch] + mm(wl[1], agg)
         s = jax.nn.sigmoid(preact)
+        slope = s * (1.0 + preact * (1.0 - s))
+        pre[ch, CF:] = slope[CF:]
+        cot = jnp.concatenate([cotb[ch, t] for t in order[:2]], axis=0)
+        gpb[ch, :CF] = (cot.astype(F32) * slope[:CF]).astype(BF16)
         result = (preact[:CF] * s[:CF]).astype(BF16)
         out_o[:, cut] = result[:F]
         outm[ch] = result[F:]
-        slope = s * (1.0 + preact * (1.0 - s))
-        wait_cot(ch)
-        cot = jnp.concatenate([cotb[ch, t] for t in order], axis=0)
-        gp = (cot.astype(F32) * slope).astype(BF16)
-        gpb[ch] = gp
+        rcopy(outm.at[ch], out_o.at[:, cut], om_s, om_r, d, mate).start()
+        both = jnp.concatenate([stacked_x(ch), agg], axis=0)
+        grads = grads + mm_nt(gpb[ch, :CF], both)
+    gown[...] = grads[:F]
+    gmate[...] = grads[F:]
+    grad_copy = rcopy(gmate, gin, gm_s, gm_r, d, mate)
+    grad_copy.start()
+    back_left = jnp.concatenate([wb[0, c], wb[0, 1 - c], wb[1, c], wb[1, 1 - c]], axis=0)
+
+    def back_chunk(ch):
+        for q in range(1, G):
+            t = lax.rem(g - q + G, G) * 2
+            came(cotb.at[ch, pl.ds(t, 2)], cx_r.at[q - 1, ch])
+        cut = half_cut(c, ch)
+        cot = jnp.concatenate([cotb[ch, t] for t in order[2:]], axis=0)
+        gpb[ch, CF:] = (cot.astype(F32) * pre[ch, CF:]).astype(BF16)
         back = mm(back_left, gpb[ch])
         at = pl.ds(c * BH + ch * CB, CB)
         for i in range(CB):
@@ -500,24 +473,32 @@
                 BF16
             )
             scm[ch, i] = (back[CF + F :, lane] * inverse).astype(BF16)
-        scaled_copies.append(
-            go(rcopy(scm.at[ch], scaled.at[at], sm_s.at[ch], sm_r.at[ch], d, mate))
-        )
+        rcopy(scm.at[ch], scaled.at[at], sm_s, sm_r, d, mate).start()
         acc_o[:, cut] = back[:F]
         accm[ch] = back[F:CF]
-        acc_copies.append(
-            go(rcopy(accm.at[ch], acc_o.at[:, cut], am_s.at[ch], am_r.at[ch], d, mate))
-        )
-        out_copies.append(
-            go(rcopy(outm.at[ch], out_o.at[:, cut], om_s.at[ch], om_r.at[ch], d, mate))
-        )
-        both = jnp.concatenate([stacked_x(ch), agg], axis=0)
-        grads = grads + mm_nt(gpb[ch, :CF], both)
-    gmate[...] = grads[F:]
-    grad_copy = go(rcopy(gmate, gin, gm_s, gm_r, d, mate))
-
-    for copy in scaled_copies:
-        copy.wait_recv()
+        rcopy(accm.at[ch], acc_o.at[:, cut], am_s, am_r, d, mate).start()
+
+    rows = F // D
+    for ch in range(CHUNKS):
+        if ch == 1:
+            grad_copy.wait_recv()
+            own = gown[...] + gin[...]
+            for p in range(D):
+                for i in range(2):
+                    for q in range(G):
+                        to = pl.ds(pl.multiple_of(i * RF + chips[q] * CF, CF), CF)
+                        lane = slice(i * RF + q * CF, i * RF + (q + 1) * CF)
+                        gw[p, :, to] = own[p * rows : (p + 1) * rows, lane]
+
+            def send_piece(p, carry):
+                to = ahead(p)
+                rcopy(gw.at[to], gpart.at[p], p_s, p_r, to, r).start()
+                return carry
+
+            lax.fori_loop(1, D, send_piece, 0)
+        back_chunk(ch)
+
+    came(scm, sm_r)
 
     def away(p, dst, slot):
         source = ahead(p)
@@ -525,36 +506,27 @@
             block = scaled[rrows[k, source]]
             dst[slot, k] = mm(block, rtiles[source, k]).astype(BF16)
 
-    def returned(p):
-        return rcopy(ret.at[p], back_o.at[d], b_s.at[p], b_r.at[p], ahead(p), r)
-
     def send_back(p, carry):
         away(p, ret, p)
-        returned(p).start()
+        rcopy(ret.at[p], back_o.at[d], b_s, b_r, ahead(p), r).start()
         return carry
 
     lax.fori_loop(1, D, send_back, 0, unroll=7)
     away(0, back_o, d)
 
-    rows = F // D
-    grad_copy.wait_recv()
-    own = grads[:F] + gin[...]
-    for p in range(D):
-        for i in range(2):
-            for q in range(G):
-                to = pl.ds(pl.multiple_of(i * RF + chips[q] * CF, CF), CF)
-                lane = slice(i * RF + q * CF, i * RF + (q + 1) * CF)
-                gw[p, :, to] = own[p * rows : (p + 1) * rows, lane]
-
-    def piece(p):
-        to = ahead(p)
-        return rcopy(gw.at[to], gpart.at[p], p_s.at[p], p_r.at[p], to, r)
-
-    def send_piece(p, carry):
-        piece(p).start()
+    came(gpart.at[others], p_r)
+
+    def take_piece(p, total):
+        return total + gpart[p]
+
+    red[...] = lax.fori_loop(1, D, take_piece, gw[d])
+
+    def send_final(p, carry):
+        rcopy(red, final_o.at[d], f_s, f_r, ahead(p), r).start()
         return carry
 
-    lax.fori_loop(1, D, send_piece, 0)
+    lax.fori_loop(1, D, send_final, 0)
+    final_o[d] = red[...]
 
     def near_back(b, carry):
         right = jnp.concatenate([ltiles[b, l] for l in range(L)], axis=1)
@@ -564,8 +536,7 @@
         return carry
 
     lax.fori_loop(0, B, near_back, 0, unroll=4)
-    for copy in acc_copies:
-        copy.wait_recv()
+    came(accm, am_r)
 
     def gather_back(block, carry):
         at = pl.ds(pl.multiple_of(block * T, T), T)
@@ -578,38 +549,28 @@
         acc_o[:, at] = lax.fori_loop(0, B, add, acc_o[:, at], unroll=8)
         return carry
 
-    lax.fori_loop(0, BH, gather_back, 0)
-
-    def take_piece(p, total):
-        piece(p).wait_recv()
-        return total + gpart[p]
-
-    red[...] = lax.fori_loop(1, D, take_piece, gw[d])
-
-    def final(p):
-        return rcopy(red, final_o.at[d], f_s.at[p], f_r.at[p], ahead(p), r)
-
-    def send_final(p, carry):
-        final(p).start()
-        return carry
-
-    lax.fori_loop(1, D, send_final, 0)
-    final_o[d] = red[...]
-    lax.fori_loop(BH, B, gather_back, 0)
-    for copy in out_copies:
-        copy.wait_recv()
-
-    def drain(p, carry):
-        for q in range(G):
-            halo(q, p).wait_send()
-            halo_on(q, p).wait_send()
-        returned(p).wait()
-        piece(p).wait_send()
-        final(p).wait()
-        return carry
-
-    lax.fori_loop(1, D, drain, 0)
-    for copy in sends:
+    lax.fori_loop(0, B, gather_back, 0)
+
+    came(ret.at[others], b_r)
+    came(gpart.at[others], f_r)
+    came(outm, om_r)
+    went(ret.at[others], b_s)
+    went(gpart.at[others], p_s)
+    went(gpart.at[others], f_s)
+    went(outm, om_s)
+    went(accm, am_s)
+    went(scm, sm_s)
+    grad_copy.wait_send()
+    went(cotb.at[pl.ds(0, CHUNKS), r], cm_s)
+    mate_feat.wait_send()
+    for q in range(1, G):
+        went(fown, xs_s.at[q - 1])
+        went(fown, xf_s.at[q - 1])
+        went(cot_h, cx_s.at[q - 1])
+    for q in range(G):
+        went(hsend.at[q, others], h_s.at[q])
+        halo_on(q).wait_send()
+    for copy in weight_copies:
         copy.wait_send()
 
 
@@ -703,49 +664,51 @@
             pltpu.VMEM((CHUNKS, CB, F, T), BF16),
             pltpu.VMEM((F, 2 * RF), F32),
             pltpu.VMEM((F, 2 * RF), F32),
+            pltpu.VMEM((F, 2 * RF), F32),
             pltpu.VMEM((D, rows, 2 * RF), F32),
             pltpu.VMEM((D, rows, 2 * RF), F32),
             pltpu.VMEM((rows, 2 * RF), F32),
             pltpu.VMEM((D, K, F, T), BF16),
             pltpu.VMEM((L, B, F, T), F32),
             pltpu.SMEM((S,), jnp.int32),
+            pltpu.SMEM((S,), jnp.int32),
             pltpu.SMEM((BH,), jnp.int32),
-            dma((B,)),
+            dma,
             dma,
             dma((M,)),
+            dma,
+            dma,
             dma((2,)),
-            dma((CHUNKS,)),
-            dma((2,)),
-            dma((G, PIECES)),
-            dma((G, PIECES)),
-            dma,
-            dma,
-            dma((G, PIECES)),
-            dma((G, PIECES)),
-            dma((G, D)),
-            dma((G, D)),
-            dma((G, D)),
-            dma((G, D)),
-            dma((R,)),
-            dma((R,)),
-            dma((CHUNKS,)),
-            dma((CHUNKS,)),
-            dma((G, 2, CHUNKS)),
-            dma((G, 2, CHUNKS)),
-            dma((CHUNKS,)),
-            dma((CHUNKS,)),
-            dma((CHUNKS,)),
-            dma((CHUNKS,)),
-            dma((CHUNKS,)),
-            dma((CHUNKS,)),
-            dma,
-            dma,
-            dma((D,)),
-            dma((D,)),
-            dma((D,)),
-            dma((D,)),
-            dma((D,)),
-            dma((D,)),
+            dma((M,)),
+            dma((M, PIECES)),
+            dma,
+            dma,
+            dma((M,)),
+            dma((M,)),
+            dma((G,)),
+            dma((G,)),
+            dma((G,)),
+            dma((G,)),
+            dma((2 * G - 1,)),
+            dma((2 * G - 1,)),
+            dma,
+            dma,
+            dma((M,)),
+            dma((M, CHUNKS)),
+            dma,
+            dma,
+            dma,
+            dma,
+            dma,
+            dma,
+            dma,
+            dma,
+            dma,
+            dma,
+            dma,
+            dma,
+            dma,
+            dma,
         ],
         compiler_params=pltpu.CompilerParams(
             collective_id=0, has_side_effects=True, vmem_limit_bytes=limit

time: 58.8 us -> 48.4 us (0.82)
  Pallas kernels: 58 us -> 47.6 us
    pallas_call x1, Pallas kernels: 55.8 us -> 45.4 us  [local(): pl.pallas_call(functools.partial(main_kernel, D, R), out_shape=(pltpu.VME...]
where the time goes in v3:
time: 48.4 us; the launch traced here: 48.2 us
  Pallas kernels  47.6 us (98%)
  between operations  0.66 us (1%)
    pallas_call x1, Pallas kernels, local(): pl.pallas_call(functools.partial(main_kernel, D, R), out_shape=(pltpu.VME...  45.4 us
    pallas_call x1, Pallas kernels, local(): pl.pallas_call(finish_kernel, out_shape=(jax.ShapeDtypeStruct((F, N), BF1...  2.17 us

profile of v3, /device:TPU:0, one launch (start us, length us, event | category | flops | bytes accessed | tf_op | source)
XLA Modules:
  0.0 48.2 jit_solution(4469863856180330834)
XLA Ops:
  0.6 0.0 copy-start
  0.6 45.4 %layer_main.1 = (bf16[64,4096]{1,0:T(8,128)(2,1)S(1)}, f32[64,4096]{1,0:T(8,128)S(1)}, bf16[8,2,64,128]{3,2,1,0:T(8,128)(2,1)S(1)}, f32[8,8,512]{2,1,0:T(8,128)S(1)}) custom-call(bf16[64,4096]{1,0:T(8,128)(2,1)} %feats_h.1, bf16[64,256]{1,0:T(8,128)(2,1)} %bitcast.15, bf16[64,256]{1,0:T(8,128)(2,1)} %bitcast.16, s32[2,32]{1,0:T(2,128)} %bitcast.17, ...), custom_call_target="tpu_custom_call" | custom-call | tf_op jit(solution)/shard_map/layer_main/pallas_call | solution.py:632
  46.0 0.0 copy-done
  46.1 2.2 %finish.1 = (bf16[64,4096]{1,0:T(8,128)(2,1)}, bf16[64,4096]{1,0:T(8,128)(2,1)}, f32[64,256]{1,0:T(8,128)}, f32[64,256]{1,0:T(8,128)}) custom-call(s32[2,8]{1,0:T(2,128)S(1)} %bitcast.13, f32[64,4096]{1,0:T(8,128)S(1)} %get-tuple-element.12.acc, bf16[8,2,64,128]{3,2,1,0:T(8,128)(2,1)S(1)} %get-tuple-element.13.back, ...), custom_call_target="tpu_custom_call" | custom-call | tf_op jit(solution)/shard_map/finish/pallas_call | solution.py:728
Async XLA Ops:
  0.6 45.4 %copy-start = (s32[1,8,2]{1,2,0:T(2,128)S(1)}, s32[1,8,2]{1,2,0:T(2,128)}, u32[]{:S(2)}) copy-start(s32[1,8,2]{1,2,0:T(2,128)} %param.14) | copy-start | bytes 196

commit v4 on v3

--- a/solution.py
+++ b/solution.py
@@ -23,15 +23,6 @@
 
 def mm_nt(a, b):
     return lax.dot_general(a, b, NT, preferred_element_type=F32)
-
-
-def equal_int(x, y):
-    gap = x - y
-    return 1 - jnp.minimum(gap * gap, 1)
-
-
-def equal_one(x, y):
-    return equal_int(x, y).astype(F32)
 
 
 def rcopy(src, dst, send, recv, dom, rep):
@@ -51,16 +42,25 @@
     feats_h,
     wts_h,
     wtn_h,
-    cols,
-    slist,
-    rrows,
+    cols_h,
+    slist_h,
+    rrows_h,
     ltiles_h,
     rtiles_h,
     cot_h,
     out_o,
-    acc_o,
-    back_o,
+    gf_o,
     final_o,
+    cols,
+    slist,
+    rrows,
+    colv,
+    slistv,
+    rrowv,
+    tabv,
+    tab,
+    acc,
+    got,
     fown,
     fmir,
     xchip,
@@ -86,14 +86,15 @@
     gown,
     gmate,
     gin,
+    gsum,
     gw,
     gpart,
     red,
     ret,
-    nearb,
-    rowtab,
-    prev,
-    last,
+    nchain,
+    hchain,
+    i_l,
+    tab_l,
     f_l,
     own_l,
     mir_l,
@@ -138,7 +139,7 @@
     F, N = feats_h.shape
     B, L, T, _ = ltiles.shape
     K = slist.shape[0]
-    RF, CF, S = R * F, 2 * F, D * K
+    RF, CF = R * F, 2 * F
     BH, NH = B // 2, N // 2
     CB = BH // CHUNKS
     CH = CB * T
@@ -173,6 +174,19 @@
         pl.semaphore_signal(
             barrier, inc=1, device_id={"dom": dom, "rep": rep}, device_id_type=MESH
         )
+    index_loads = [
+        pltpu.make_async_copy(src, dst, i_l.at[i])
+        for i, (src, dst) in enumerate(
+            (
+                (slist_h, slist),
+                (rrows_h, rrows),
+                (cols_h, cols),
+                (cols_h, colv),
+                (rrows_h, rrowv),
+                (slist_h, slistv),
+            )
+        )
+    ]
     loads = [
         pltpu.make_async_copy(feats_h.at[:, b * T : (b + 1) * T], fown.at[b], f_l)
         for b in range(B)
@@ -190,21 +204,22 @@
         pltpu.make_async_copy(cot_h.at[:, half_cut(c, ch)], cotb.at[ch, r], c_l)
         for ch in range(CHUNKS)
     ]
-    for load in loads:
+    for load in index_loads + loads:
         load.start()
-    taken(fown, f_l)
     pl.semaphore_wait(barrier, len(greeted))
 
     for j in range(PIECES):
         for q in range(1, G):
-            rcopy(
-                fown.at[piece_cut(j)],
-                fmir.at[G - q - 1, piece_cut(j)],
-                xs_s.at[q - 1],
-                xs_r.at[G - q - 1, j],
-                d,
-                peer(q, c),
-            ).start()
+            for b in range(j * PB, (j + 1) * PB):
+                rcopy(
+                    feats_h.at[:, b * T : (b + 1) * T],
+                    fmir.at[G - q - 1, b],
+                    xs_s.at[q - 1],
+                    xs_r.at[G - q - 1, j],
+                    d,
+                    peer(q, c),
+                ).start()
+    taken(fown, f_l)
     mate_feat = rcopy(fown, xchip.at[c], xm_s, xm_r, d, mate)
     mate_feat.start()
 
@@ -214,7 +229,7 @@
             for k in range(K):
                 hsend[q, p, k] = ref(slist[k, to])
             rcopy(
-                hsend.at[q, p], hx.at[q, c, p], h_s.at[q], h_r.at[q], to, r
+                hsend.at[q, p], hx.at[q, c, p], h_s.at[q], h_r.at[q, p], to, r
             ).start()
             return carry
 
@@ -227,9 +242,15 @@
         return rcopy(part, part, hf_s.at[q], hf_r.at[q], d, mate)
 
     def pass_halo(q):
-        came(hx.at[q, c, others], h_r.at[q])
-        halo_on(q).start()
-
+        def step(p, carry):
+            part = hx.at[q, c, p]
+            came(part, h_r.at[q, p])
+            rcopy(part, part, hf_s.at[q], hf_r.at[q], d, mate).start()
+            return carry
+
+        lax.fori_loop(1, D, step, 0)
+
+    index_loads[0].wait()
     send_halos(0, lambda block: fown[block])
     own_copy = pltpu.make_async_copy(fown, xchip.at[c], own_l)
     own_copy.start()
@@ -279,28 +300,31 @@
         lax.fori_loop(0, BH, step, 0, unroll=4)
 
     def far(q):
-        def step(p, carry):
-            source = lax.rem(d - p + D, D)
+        def step(source, carry):
+            p = lax.rem(d - source + D, D)
             high = CF + KEEP if q == 0 else CF
             for k in range(K):
-                s = p * K + k
                 left = [hx[q, core, p, k] for core in range(2)]
                 if q == 0:
                     left.append(ones)
                 term = mm_nt(jnp.concatenate(left, axis=0), rtiles[source, k])[:high]
-                chain[q, s + 1, :high] = term + chain[q, prev[s], :high]
+                before = tab[row_tab + 2 * k, source]
+                chain[k, source + 1, :high] = term + chain[k, before, :high]
             return carry
 
         lax.fori_loop(0, D, step, 0, unroll=4)
 
     def place(q):
         def step(i, carry):
+            high = CF + KEEP if q == 0 else CF
+            total = sums[q, i, :high]
+            for k in range(K):
+                end = tab[row_tab + 2 * k + 1, c * BH + i]
+                total = total + chain[k, end, :high]
             if q == 0:
-                total = sums[q, i] + chain[q, last[i]]
                 inverse = 1.0 / (1.0 + total[CF:])
                 inv[i] = inverse
             else:
-                total = sums[q, i, :CF] + chain[q, last[i], :CF]
                 inverse = inv[i]
             xa[q, i] = (total[:CF] * inverse[:1]).astype(BF16)
             return carry
@@ -320,6 +344,33 @@
                 mate,
             ).start()
 
+    for load in index_loads[1:]:
+        load.wait()
+    near_tab, row_tab, home_tab = 0, 2 * L, 2 * L + 2 * K
+
+    def make_tables(first, ref, count):
+        n = ref.shape[1]
+        size = max(n, B)
+        entry = lax.broadcasted_iota(jnp.int32, (n, size), 0)
+        place_of = lax.broadcasted_iota(jnp.int32, (n, size), 1)
+        for i in range(count):
+            across = jnp.broadcast_to(ref[i : i + 1, :], (n, n))
+            down = across.astype(F32).T.astype(jnp.int32)
+            older = (across == down) & (entry[:, :n] < place_of[:, :n])
+            before = jnp.max(jnp.where(older, entry[:, :n] + 1, 0), axis=0)
+            wide = jnp.broadcast_to(down[:, :1], (n, size))
+            end = jnp.max(jnp.where(wide == place_of, entry + 1, 0), axis=0)
+            tabv[first + 2 * i, :n] = before
+            tabv[first + 2 * i + 1, :size] = end
+
+    make_tables(near_tab, colv, L)
+    make_tables(row_tab, rrowv, K)
+    make_tables(home_tab, slistv, K)
+    tab_copy = pltpu.make_async_copy(tabv, tab, tab_l)
+    tab_copy.start()
+    chain[:, 0] = jnp.zeros((K, CF + KEEP, T), F32)
+    nchain[:, 0] = jnp.zeros((L, F, T), F32)
+    hchain[:, 0] = jnp.zeros((K, F, T), F32)
     own_copy.wait()
     mate_feat.wait_recv()
     for k in range(K):
@@ -329,36 +380,7 @@
     near(0, lambda core, col: xchip[core, col])
     tile_loads[1].wait()
 
-    def list_rows(p, carry):
-        source = lax.rem(d - p + D, D)
-        for k in range(K):
-            rowtab[p * K + k] = rrows[k, source]
-        return carry
-
-    lax.fori_loop(0, D, list_rows, 0)
-
-    def previous(s, carry):
-        row = rowtab[s]
-
-        def look(j, found):
-            before = jnp.minimum(jnp.maximum(s - j, 0), 1)
-            return jnp.maximum(found, (j + 1) * before * equal_int(row, rowtab[j]))
-
-        prev[s] = lax.fori_loop(0, S, look, 0, unroll=16)
-        return carry
-
-    lax.fori_loop(0, S, previous, 0)
-
-    def latest(i, carry):
-        def look(j, found):
-            return jnp.maximum(found, (j + 1) * equal_int(c * BH + i, rowtab[j]))
-
-        last[i] = lax.fori_loop(0, S, look, 0, unroll=16)
-        return carry
-
-    lax.fori_loop(0, BH, latest, 0)
-    for q in range(G):
-        chain[q, 0] = jnp.zeros((CF + KEEP, T), F32)
+    tab_copy.wait()
     pass_feats(0)
     pass_halo(0)
     for j in range(1, PIECES - 1):
@@ -474,13 +496,13 @@
             )
             scm[ch, i] = (back[CF + F :, lane] * inverse).astype(BF16)
         rcopy(scm.at[ch], scaled.at[at], sm_s, sm_r, d, mate).start()
-        acc_o[:, cut] = back[:F]
+        acc[:, cut] = back[:F]
         accm[ch] = back[F:CF]
-        rcopy(accm.at[ch], acc_o.at[:, cut], am_s, am_r, d, mate).start()
+        rcopy(accm.at[ch], acc.at[:, cut], am_s, am_r, d, mate).start()
 
     rows = F // D
     for ch in range(CHUNKS):
-        if ch == 1:
+        if ch == CHUNKS - 1:
             grad_copy.wait_recv()
             own = gown[...] + gin[...]
             for p in range(D):
@@ -488,7 +510,8 @@
                     for q in range(G):
                         to = pl.ds(pl.multiple_of(i * RF + chips[q] * CF, CF), CF)
                         lane = slice(i * RF + q * CF, i * RF + (q + 1) * CF)
-                        gw[p, :, to] = own[p * rows : (p + 1) * rows, lane]
+                        gsum[p, :, to] = own[p * rows : (p + 1) * rows, lane]
+                gw[p] = gsum[p].astype(BF16)
 
             def send_piece(p, carry):
                 to = ahead(p)
@@ -508,18 +531,18 @@
 
     def send_back(p, carry):
         away(p, ret, p)
-        rcopy(ret.at[p], back_o.at[d], b_s, b_r, ahead(p), r).start()
+        rcopy(ret.at[p], got.at[d], b_s, b_r, ahead(p), r).start()
         return carry
 
-    lax.fori_loop(1, D, send_back, 0, unroll=7)
-    away(0, back_o, d)
+    early = (D + 1) // 2
+    lax.fori_loop(1, early, send_back, 0, unroll=3)
 
     came(gpart.at[others], p_r)
 
     def take_piece(p, total):
-        return total + gpart[p]
-
-    red[...] = lax.fori_loop(1, D, take_piece, gw[d])
+        return total + gpart[p].astype(F32)
+
+    red[...] = lax.fori_loop(1, D, take_piece, gsum[d]).astype(BF16)
 
     def send_final(p, carry):
         rcopy(red, final_o.at[d], f_s, f_r, ahead(p), r).start()
@@ -527,31 +550,49 @@
 
     lax.fori_loop(1, D, send_final, 0)
     final_o[d] = red[...]
+    lax.fori_loop(early, D, send_back, 0, unroll=4)
+    away(0, got, d)
 
     def near_back(b, carry):
         right = jnp.concatenate([ltiles[b, l] for l in range(L)], axis=1)
         both = mm(scaled[b], right)
         for l in range(L):
-            nearb[l, b] = both[:, l * T : (l + 1) * T]
+            before = tab[near_tab + 2 * l, b]
+            nchain[l, b + 1] = both[:, l * T : (l + 1) * T] + nchain[l, before]
         return carry
 
     lax.fori_loop(0, B, near_back, 0, unroll=4)
     came(accm, am_r)
 
-    def gather_back(block, carry):
+    def gather_near(block, carry):
         at = pl.ds(pl.multiple_of(block * T, T), T)
-
-        def add(i, total):
-            for l in range(L):
-                total = total + nearb[l, i] * equal_one(cols[l, i], block)
-            return total
-
-        acc_o[:, at] = lax.fori_loop(0, B, add, acc_o[:, at], unroll=8)
+        total = acc[:, at]
+        for l in range(L):
+            total = total + nchain[l, tab[near_tab + 2 * l + 1, block]]
+        acc[:, at] = total
         return carry
 
-    lax.fori_loop(0, B, gather_back, 0)
+    lax.fori_loop(0, B, gather_near, 0, unroll=4)
 
     came(ret.at[others], b_r)
+    def home(s, carry):
+        for k in range(K):
+            before = tab[home_tab + 2 * k, s]
+            hchain[k, s + 1] = got[s, k].astype(F32) + hchain[k, before]
+        return carry
+
+    lax.fori_loop(0, D, home, 0, unroll=4)
+
+    def gather_home(block, carry):
+        at = pl.ds(pl.multiple_of(block * T, T), T)
+        total = acc[:, at]
+        for k in range(K):
+            total = total + hchain[k, tab[home_tab + 2 * k + 1, block]]
+        gf_o[:, at] = total.astype(BF16)
+        return carry
+
+    lax.fori_loop(0, B, gather_home, 0, unroll=4)
+
     came(gpart.at[others], f_r)
     came(outm, om_r)
     went(ret.at[others], b_s)
@@ -574,28 +615,18 @@
         copy.wait_send()
 
 
-def finish_kernel(slist, acc, back, final, out_v, out_o, gf_o, gs_o, gn_o, total, sem):
-    store = pltpu.make_async_copy(out_v, out_o, sem)
-    store.start()
-    total[...] = acc[...]
-    D, K, _, T = back.shape
-    _, rows, width = final.shape
-    half = width // 2
-
-    def home(s, carry):
-        for k in range(K):
-            at = pl.ds(pl.multiple_of(slist[k, s] * T, T), T)
-            total[:, at] = total[:, at] + back[s, k].astype(F32)
-        return carry
-
-    lax.fori_loop(0, D, home, 0)
-    gf_o[...] = total[...].astype(BF16)
-    for p in range(D):
-        part = final[p]
-        where = slice(p * rows, (p + 1) * rows)
-        gs_o[where, :] = part[:, :half]
-        gn_o[where, :] = part[:, half:]
-    store.wait()
+def finish_kernel(final, out_v, gf_v, out_o, gf_o, gs_o, gn_o, sem):
+    stores = [
+        pltpu.make_async_copy(src, dst, sem.at[i])
+        for i, (src, dst) in enumerate(((out_v, out_o), (gf_v, gf_o)))
+    ]
+    for store in stores:
+        store.start()
+    half = gs_o.shape[2]
+    gs_o[...] = final[:, :, :half].astype(F32)
+    gn_o[...] = final[:, :, half:].astype(F32)
+    for store in stores:
+        store.wait()
 
 
 def local(
@@ -615,31 +646,40 @@
     B, L, T, _ = local_tiles.shape
     K = send_list.shape[2]
     G = R // 2
-    RF, CF, S = R * F, 2 * F, D * K
+    RF, CF = R * F, 2 * F
     BH = B // 2
     CB = BH // CHUNKS
     CH = CB * T
     rows = F // D
     M = max(G - 1, 1)
+    tables = -(-(2 * L + 4 * K) // 8) * 8
     vmem = pl.BlockSpec(memory_space=pltpu.VMEM)
-    smem = pl.BlockSpec(memory_space=pltpu.SMEM)
     hbm = pl.BlockSpec(memory_space=pltpu.HBM)
     dma = pltpu.SemaphoreType.DMA
     slist = jnp.swapaxes(send_list, 1, 2)[0]
     rrows = jnp.swapaxes(remote_rows, 1, 2)[0]
     far_tiles = remote_tiles[0]
     limit = 56 * 1024 * 1024
-    output, acc, back, final = pl.pallas_call(
+    output, grad_feats, final = pl.pallas_call(
         functools.partial(main_kernel, D, R),
         out_shape=(
             pltpu.VMEM((F, N), BF16),
+            pltpu.VMEM((F, N), BF16),
+            pltpu.VMEM((D, rows, 2 * RF), BF16),
+        ),
+        in_specs=[hbm] * 9,
+        out_specs=(vmem, vmem, vmem),
+        scratch_shapes=[
+            pltpu.SMEM((L, B), jnp.int32),
+            pltpu.SMEM((K, D), jnp.int32),
+            pltpu.SMEM((K, D), jnp.int32),
+            pltpu.VMEM((L, B), jnp.int32),
+            pltpu.VMEM((K, D), jnp.int32),
+            pltpu.VMEM((K, D), jnp.int32),
+            pltpu.VMEM((tables, T), jnp.int32),
+            pltpu.SMEM((tables, T), jnp.int32),
             pltpu.VMEM((F, N), F32),
             pltpu.VMEM((D, K, F, T), BF16),
-            pltpu.VMEM((D, rows, 2 * RF), F32),
-        ),
-        in_specs=[hbm, hbm, hbm, smem, smem, smem, hbm, hbm, hbm],
-        out_specs=(vmem, vmem, vmem, vmem),
-        scratch_shapes=[
             pltpu.VMEM((B, F, T), BF16),
             pltpu.VMEM((M, B, F, T), BF16),
             pltpu.VMEM((2, B, F, T), BF16),
@@ -653,7 +693,7 @@
             pltpu.VMEM((G, D, K, F, T), BF16),
             pltpu.VMEM((G, 2, D, K, F, T), BF16),
             pltpu.VMEM((G, BH, CF + KEEP, T), F32),
-            pltpu.VMEM((G, S + 1, CF + KEEP, T), F32),
+            pltpu.VMEM((K, D + 1, CF + KEEP, T), F32),
             pltpu.VMEM((BH, KEEP, T), F32),
             pltpu.VMEM((G, BH, CF, T), BF16),
             pltpu.VMEM((CHUNKS, RF, CH), F32),
@@ -666,13 +706,14 @@
             pltpu.VMEM((F, 2 * RF), F32),
             pltpu.VMEM((F, 2 * RF), F32),
             pltpu.VMEM((D, rows, 2 * RF), F32),
-            pltpu.VMEM((D, rows, 2 * RF), F32),
-            pltpu.VMEM((rows, 2 * RF), F32),
+            pltpu.VMEM((D, rows, 2 * RF), BF16),
+            pltpu.VMEM((D, rows, 2 * RF), BF16),
+            pltpu.VMEM((rows, 2 * RF), BF16),
             pltpu.VMEM((D, K, F, T), BF16),
-            pltpu.VMEM((L, B, F, T), F32),
-            pltpu.SMEM((S,), jnp.int32),
-            pltpu.SMEM((S,), jnp.int32),
-            pltpu.SMEM((BH,), jnp.int32),
+            pltpu.VMEM((L, B + 1, F, T), F32),
+            pltpu.VMEM((K, D + 1, F, T), F32),
+            dma((6,)),
+            dma,
             dma,
             dma,
             dma((M,)),
@@ -686,7 +727,7 @@
             dma((M,)),
             dma((M,)),
             dma((G,)),
-            dma((G,)),
+            dma((G, D)),
             dma((G,)),
             dma((G,)),
             dma((2 * G - 1,)),
@@ -730,16 +771,16 @@
         out_shape=(
             jax.ShapeDtypeStruct((F, N), BF16),
             jax.ShapeDtypeStruct((F, N), BF16),
-            jax.ShapeDtypeStruct((F, RF), F32),
-            jax.ShapeDtypeStruct((F, RF), F32),
+            jax.ShapeDtypeStruct((D, rows, RF), F32),
+            jax.ShapeDtypeStruct((D, rows, RF), F32),
         ),
-        in_specs=[smem, vmem, vmem, vmem, vmem],
-        out_specs=(hbm, vmem, vmem, vmem),
-        scratch_shapes=[pltpu.VMEM((F, N), F32), dma],
+        in_specs=[vmem, vmem, vmem],
+        out_specs=(hbm, hbm, vmem, vmem),
+        scratch_shapes=[dma((2,))],
         compiler_params=pltpu.CompilerParams(vmem_limit_bytes=24 * 1024 * 1024),
         name="finish",
-    )(slist, acc, back, final, output)
-    return output, grad_feats, gs.T, gn.T
+    )(final, output, grad_feats)
+    return output, grad_feats, gs.reshape(F, RF).T, gn.reshape(F, RF).T
 
 
 def solution(mesh):

time: 48.4 us -> 43.9 us (0.907)
  Pallas kernels: 47.6 us -> 43.1 us
    pallas_call x1, Pallas kernels: 45.4 us -> 41.4 us  [local(): pl.pallas_call(functools.partial(main_kernel, D, R), out_shape=(pltpu.VME...]
    pallas_call x1, Pallas kernels: 2.17 us -> 1.64 us  [local(): pl.pallas_call(finish_kernel, out_shape=(jax.ShapeDtypeStruct((F, N), BF1...]
where the time goes in v4:
time: 43.9 us; the launch traced here: 43.7 us
  Pallas kernels  43.1 us (98%)
  between operations  0.64 us (1%)
    pallas_call x1, Pallas kernels, local(): pl.pallas_call(functools.partial(main_kernel, D, R), out_shape=(pltpu.VME...  41.4 us
    pallas_call x1, Pallas kernels, local(): pl.pallas_call(finish_kernel, out_shape=(jax.ShapeDtypeStruct((F, N), BF1...  1.64 us

profile of v4, /device:TPU:0, one launch (start us, length us, event | category | flops | bytes accessed | tf_op | source)
XLA Modules:
  0.0 43.7 jit_solution(15205893808473703932)
XLA Ops:
  0.6 41.4 %layer_main.1 = (bf16[64,4096]{1,0:T(8,128)(2,1)S(1)}, bf16[64,4096]{1,0:T(8,128)(2,1)S(1)}, bf16[8,8,512]{2,1,0:T(8,128)(2,1)S(1)}) custom-call(bf16[64,4096]{1,0:T(8,128)(2,1)} %feats_h.1, bf16[64,256]{1,0:T(8,128)(2,1)} %bitcast.17, bf16[64,256]{1,0:T(8,128)(2,1)} %bitcast.18, s32[2,32]{1,0:T(2,128)} %bitcast.19, s32[2,8]{1,0:T(2,128)} %bitcast.20, ...), custom_call_target="tpu_custom_call" | custom-call | tf_op jit(solution)/shard_map/layer_main/pallas_call | solution.py:663
  42.1 1.6 %finish.1 = (bf16[64,4096]{1,0:T(8,128)(2,1)}, bf16[64,4096]{1,0:T(8,128)(2,1)}, f32[8,8,256]{2,1,0:T(8,128)}, f32[8,8,256]{2,1,0:T(8,128)}) custom-call(bf16[8,8,512]{2,1,0:T(8,128)(2,1)S(1)} %get-tuple-element.11.final, bf16[64,4096]{1,0:T(8,128)(2,1)S(1)} %get-tuple-element.12.out_v, bf16[64,4096]{1,0:T(8,128)(2,1)S(1)} %get-tuple-element.13.gf_v), custom_call_target="tpu_custom_call" | custom-call | tf_op jit(solution)/shard_map/finish/pallas_call | solution.py:769
